TPU v7x, 32 devices: a whole 2x2x4 slice. The times are simulated.
32 devices in a mesh: dp: 4 (over z), cent: 8 (over y, x, core).
Axes of the slice: x: 2, y: 2, z: 4, core: 2. Of those that a mesh axis runs over, the one named last changes fastest.
Arguments:
- vectors: bfloat16 [8192, 768], P('dp'), may hold values from -30 to 30
- centroids: bfloat16 [16384, 768], P('cent'), may hold values from -1 to 1
- assignment: int32 [8192], P(('dp', 'cent')), may hold values from 0 to 16383, as said below
Outputs:
- new_centroids: bfloat16 [16384, 768], P('cent')
- row_potential: float32 [8192], P('dp')
- column_potential: float32 [16384], P('cent')
- residuals: bfloat16 [8192, 768], P(('dp', 'cent'))
Inputs may be any that keep to these rules, and one draw needn't show every extreme that they name: `assignment`: the entry's centroid is owned by index entry // 2048 of cent. In each aligned block of 256 entries (the rows of one device), at most 64 entries name centroids of one owning index; one owning index, drawn from the seed, receives exactly 64 entries from every block.
All inputs are finite; a program needn't handle non-finite values.
Results may differ from a plain program's by a relative error of at most 0.00705.
Values may be sent and summed in bfloat16 or wider, within the bound.
No kernel may reach another device: no remote copies, remote signals or barrier semaphores. Data moves between devices by JAX's collectives and lax.ppermute only.
A program may use at most 128 MiB of HBM per device.

v0:
```python
import functools
import math

import jax
import jax.numpy as jnp
from jax import lax
from jax.experimental import pallas as pl
from jax.experimental.pallas import tpu as pltpu
from jax.sharding import PartitionSpec as P


ITERS = 3


F32 = jnp.float32
BF16 = jnp.bfloat16
NT = (((1,), (1,)), ((), ()))
NN = (((1,), (0,)), ((), ()))
MIB = 1 << 20


def cost(flops, moved, exps=0):
    return pl.CostEstimate(flops=int(flops), bytes_accessed=int(moved), transcendentals=int(exps))


def grant(mib):
    return pltpu.CompilerParams(vmem_limit_bytes=mib * MIB)


def tree(parts, join):
    while len(parts) > 1:
        parts = [join(parts[k], parts[k + 1]) for k in range(0, len(parts), 2)]
    return parts[0]


def join_pairs(parts):
    peak = tree([part[0:1] for part in parts], jnp.maximum)
    total = tree([part[1:2] * jnp.exp(part[0:1] - peak) for part in parts], jnp.add)
    return peak, total


def in_hbm(value):
    return pltpu.with_memory_space_constraint(value, pltpu.HBM)


def in_vmem(value):
    return pltpu.with_memory_space_constraint(value, pltpu.VMEM)


def whole(shape):
    return pl.BlockSpec(shape, lambda *_: (0,) * len(shape))


def logits_kernel(v_ref, c_ref, l_ref, stat_ref, *, chunk):
    doubled = c_ref[...] * 2
    rows = v_ref.shape[0]
    peak, total = None, None
    for start in range(0, rows, chunk):
        part = lax.dot_general(
            v_ref[start : start + chunk, :], doubled, NT, preferred_element_type=F32
        )
        l_ref[start : start + chunk, :] = part
        part_peak = jnp.max(part, axis=0, keepdims=True)
        higher = part_peak if peak is None else jnp.maximum(peak, part_peak)
        part_total = jnp.sum(jnp.exp(part - higher), axis=0, keepdims=True)
        total = part_total if peak is None else total * jnp.exp(peak - higher) + part_total
        peak = higher
    stat_ref[0:1, :] = peak
    stat_ref[1:2, :] = total


def logits_and_stats(vectors, centroids):
    rows, width = vectors.shape
    lists = centroids.shape[0]
    tile = min(512, lists)
    return pl.pallas_call(
        functools.partial(logits_kernel, chunk=min(256, rows)),
        grid=(lists // tile,),
        in_specs=[whole((rows, width)), pl.BlockSpec((tile, width), lambda j: (j, 0))],
        out_specs=[
            pl.BlockSpec((rows, tile), lambda j: (0, j)),
            pl.BlockSpec((2, tile), lambda j: (0, j)),
        ],
        out_shape=[
            pltpu.VMEM((rows, lists), F32),
            jax.ShapeDtypeStruct((2, lists), F32),
        ],
        compiler_params=grant(24),
        cost_estimate=cost(2 * rows * lists * width, 4 * rows * lists, rows * lists),
        name="logits_stats",
    )(in_hbm(vectors), in_hbm(centroids))


def first_rows_kernel(*refs, parts, log_mass, group):
    l_ref, ids_ref = refs[0:2]
    stats = refs[2 : 2 + parts]
    m_ref, stat_ref, col_ref, peaks, totals = refs[2 + parts :]

    @pl.when(pl.program_id(0) == 0)
    def _():
        peak, total = join_pairs([part[...] for part in stats])
        col_ref[...] = log_mass - (peak + jnp.log(total))

    tile = l_ref.shape[0]

    def some(step, carry):
        rows = pl.ds(pl.multiple_of(step * group, group), group)
        shifted = l_ref[rows, :] + col_ref[...]
        peak = jnp.max(shifted, axis=1, keepdims=True)
        scaled = jnp.exp(shifted - peak)
        m_ref[rows, :] = scaled.astype(BF16)
        peaks[rows, :] = jnp.broadcast_to(peak, (group, 128))
        totals[rows, :] = jnp.broadcast_to(jnp.sum(scaled, axis=1, keepdims=True), (group, 128))
        return carry

    lax.fori_loop(0, tile // group, some, 0, unroll=4)
    stat_ref[0:1, :] = jnp.transpose(peaks[...])[0:1, :]
    stat_ref[1:2, :] = jnp.transpose(totals[...])[0:1, :]
    stat_ref[2:3, :] = ids_ref[...]


def first_rows(logits, ids, stats, log_mass):
    rows, lists = logits.shape
    tile = min(256, rows)
    return pl.pallas_call(
        functools.partial(first_rows_kernel, parts=len(stats), log_mass=log_mass, group=16),
        grid=(rows // tile,),
        in_specs=[
            pl.BlockSpec((tile, lists), lambda i: (i, 0)),
            pl.BlockSpec((1, tile), lambda i: (0, i)),
        ]
        + [whole((2, lists))] * len(stats),
        out_specs=[
            pl.BlockSpec((tile, lists), lambda i: (i, 0)),
            pl.BlockSpec((3, tile), lambda i: (0, i)),
            whole((1, lists)),
        ],
        out_shape=[
            pltpu.VMEM((rows, lists), BF16),
            jax.ShapeDtypeStruct((3, rows), F32),
            jax.ShapeDtypeStruct((1, lists), F32),
        ],
        scratch_shapes=[pltpu.VMEM((tile, 128), F32), pltpu.VMEM((tile, 128), F32)],
        compiler_params=grant(16),
        cost_estimate=cost(4 * rows * lists, 6 * rows * lists, rows * lists),
        name="first_rows",
    )(in_vmem(logits), ids, *stats)


def store_parts(where, value):
    head = value.astype(BF16)
    rest = value - head.astype(F32)
    middle = rest.astype(BF16)
    last = (rest - middle.astype(F32)).astype(BF16)
    zero = jnp.zeros((5, value.shape[1]), BF16)
    where[...] = jnp.concatenate([head, middle, last, zero], axis=0)


def add_parts(sums):
    return (sums[2:3] + sums[1:2]) + sums[0:1]


def column_sum_kernel(*refs, parts, first):
    m_ref, own_ref = refs[0:2]
    stats = refs[2 : 2 + parts]
    if first:
        out_ref, peak_ref, _, weights = refs[2 + parts :]
    else:
        peak_ref = refs[2 + parts]
        out_ref, _, weights = refs[3 + parts :]

    @pl.when(pl.program_id(0) == 0)
    def _():
        if first:
            peak, total = join_pairs([part[...] for part in stats])
            peak_ref[...] = peak
        else:
            peak = peak_ref[...]
            total = tree([part[...] for part in stats], jnp.add)
        store_parts(weights, jnp.exp(own_ref[0:1, :] - (peak + jnp.log(total))))

    out_ref[...] = add_parts(
        lax.dot_general(weights[...], m_ref[...], NN, preferred_element_type=F32)
    )


def column_sums(scaled, own, stats, peak=None):
    rows, lists = scaled.shape
    tile = min(512, lists)
    first = peak is None
    row = whole((1, rows))
    kept = pl.BlockSpec(memory_space=pl.ANY)
    out_specs = [pl.BlockSpec((1, tile), lambda j: (0, j))]
    out_shape = [jax.ShapeDtypeStruct((1, lists), F32)]
    return pl.pallas_call(
        functools.partial(column_sum_kernel, parts=len(stats), first=first),
        grid=(lists // tile,),
        in_specs=[pl.BlockSpec((rows, tile), lambda j: (0, j)), whole(own.shape)]
        + [whole(stats[0].shape)] * len(stats)
        + ([] if first else [row]),
        out_specs=out_specs + ([row] if first else []) + [kept],
        out_shape=out_shape
        + ([jax.ShapeDtypeStruct((1, rows), F32)] if first else [])
        + [pltpu.VMEM(scaled.shape, scaled.dtype)],
        input_output_aliases={0: 2 if first else 1},
        scratch_shapes=[pltpu.VMEM((8, rows), BF16)],
        compiler_params=grant(16),
        cost_estimate=cost(16 * rows * lists, 2 * rows * lists),
        name="column_sums",
    )(in_vmem(scaled), own, *stats, *([] if first else [peak]))


def row_sum_kernel(*refs, parts, ratio, log_mass):
    m_ref, first_ref, own_ref, peak_ref = refs[0:4]
    stats = refs[4 : 4 + parts]
    out_ref, col_ref, _, weights = refs[4 + parts :]

    @pl.when(pl.program_id(0) == 0)
    def _():
        total = tree([part[...] for part in stats], jnp.add)
        store_parts(weights, ratio / total)
        col_ref[...] = first_ref[...] + (log_mass - jnp.log(total))

    sums = add_parts(lax.dot_general(weights[...], m_ref[...], NT, preferred_element_type=F32))
    out_ref[...] = sums * jnp.exp(own_ref[0:1, :] - peak_ref[...])


def row_sums(scaled, first_column, own, peak, stats, ratio):
    rows, lists = scaled.shape
    tile = min(512, rows)
    column = whole((1, lists))
    return pl.pallas_call(
        functools.partial(
            row_sum_kernel, parts=len(stats), ratio=ratio, log_mass=math.log(ratio)
        ),
        grid=(rows // tile,),
        in_specs=[
            pl.BlockSpec((tile, lists), lambda i: (i, 0)),
            column,
            pl.BlockSpec((own.shape[0], tile), lambda i: (0, i)),
            pl.BlockSpec((1, tile), lambda i: (0, i)),
        ]
        + [column] * len(stats),
        out_specs=[
            pl.BlockSpec((1, tile), lambda i: (0, i)),
            column,
            pl.BlockSpec(memory_space=pl.ANY),
        ],
        out_shape=[
            jax.ShapeDtypeStruct((1, rows), F32),
            jax.ShapeDtypeStruct((1, lists), F32),
            pltpu.VMEM(scaled.shape, scaled.dtype),
        ],
        input_output_aliases={0: 2},
        scratch_shapes=[pltpu.VMEM((8, lists), BF16)],
        compiler_params=grant(16),
        cost_estimate=cost(16 * rows * lists, 2 * rows * lists),
        name="row_sums",
    )(in_vmem(scaled), first_column, own, peak, *stats)


def plan_kernel(*refs, planes, owners, depth):
    place_ref, c_ref, col_ref = refs[0:3]
    rows_in = refs[3 : 3 + planes]
    own_ref = refs[3 + planes]
    halves = refs[4 + planes : 4 + planes + 2 * (planes - 1)]
    ids_ref, out_ref = refs[4 + planes + 2 * (planes - 1) : 6 + planes + 2 * (planes - 1)]
    picked = refs[6 + planes + 2 * (planes - 1) : -6]
    held, row_all, acc, mass, chosen, sems = refs[-6:]
    tile = c_ref.shape[0]
    count = own_ref.shape[0]
    piece = count // owners
    plane, owner = place_ref[0], place_ref[1]

    def block(index):
        return pl.ds(pl.multiple_of(index * count, count), count)

    @pl.when(pl.program_id(0) == 0)
    def _():
        pltpu.make_async_copy(own_ref, held.at[block(plane)], sems.at[0]).start()
        row_all[pl.ds(plane, 1), :] = rows_in[0][...]
        for key in range(1, planes):
            other = plane ^ key
            row_all[pl.ds(other, 1), :] = rows_in[key][...]
            for index in range(owners):
                source = halves[2 * (key - 1) + index // (owners // 2)]
                at = (index % (owners // 2)) * piece
                slot = 2 * (index % (owners // 2)) + index // (owners // 2)
                start = pl.multiple_of(other * count + (owner ^ slot) * piece, piece)
                pltpu.make_async_copy(
                    source.at[pl.ds(at, piece)], held.at[pl.ds(start, piece)], sems.at[key]
                ).start()

    doubled = c_ref[...] * 2
    column = jnp.transpose(jnp.broadcast_to(col_ref[...], (128, tile)))[:, 0:1]
    steps = planes * count // depth

    def logits(step):
        here = held[step * depth : (step + 1) * depth, :]
        return lax.dot_general(doubled, here, NT, preferred_element_type=F32)

    @pl.when(pl.program_id(0) == 0)
    def _():
        for key in range(planes):
            pltpu.make_async_copy(held.at[block(key)], held.at[block(key)], sems.at[key]).wait()

    ready = logits(0)
    for step in range(steps):
        following = logits(step + 1) if step + 1 < steps else None
        start = step * depth
        row = row_all[start // count : start // count + 1, start % count : start % count + depth]
        plan = jnp.exp(ready + row + column).astype(BF16)
        part = lax.dot_general(
            plan, held[start : start + depth, :], NN, preferred_element_type=F32
        )
        wide = plan.astype(F32)
        sums = wide[:, 0:128]
        for lane in range(128, depth, 128):
            sums = sums + wide[:, lane : lane + 128]
        acc[...] = part if step == 0 else acc[...] + part
        mass[...] = sums if step == 0 else mass[...] + sums
        ready = following
    fresh = (acc[...] / jnp.sum(mass[...], axis=1, keepdims=True)).astype(BF16)
    out_ref[...] = fresh
    turn = pl.program_id(0)
    slots = ids_ref.shape[0]
    lanes = lax.broadcasted_iota(jnp.int32, (slots, tile), 1) + turn * tile
    wanted = (ids_ref[...] == lanes).astype(F32).astype(BF16)
    some = lax.dot_general(wanted, fresh, NN, preferred_element_type=F32)

    @pl.when(turn == 0)
    def _():
        chosen[...] = some

    @pl.when(turn > 0)
    def _():
        chosen[...] += some

    @pl.when(turn == pl.num_programs(0) - 1)
    def _():
        each = slots // len(picked)
        for index, piece_ref in enumerate(picked):
            piece_ref[...] = chosen[index * each : (index + 1) * each, :].astype(BF16)


def new_centroids(place, centroids, column, rows, own, halves, ids, owners):
    count, width = own.shape
    lists = centroids.shape[0]
    planes = len(rows)
    tile, depth = min(256, lists), min(1024, count)
    anywhere = pl.BlockSpec(memory_space=pl.ANY)
    total = planes * count
    return pl.pallas_call(
        functools.partial(plan_kernel, planes=planes, owners=owners, depth=depth),
        grid=(lists // tile,),
        in_specs=[
            pl.BlockSpec(memory_space=pltpu.SMEM),
            pl.BlockSpec((tile, width), lambda j: (j, 0)),
            pl.BlockSpec((1, tile), lambda j: (0, j)),
        ]
        + [whole((1, count))] * planes
        + [anywhere] * (1 + len(halves))
        + [whole(ids.shape)],
        out_specs=[pl.BlockSpec((tile, width), lambda j: (j, 0))]
        + [whole((ids.shape[0] // owners, width))] * owners,
        out_shape=[jax.ShapeDtypeStruct((lists, width), BF16)]
        + [jax.ShapeDtypeStruct((ids.shape[0] // owners, width), BF16)] * owners,
        scratch_shapes=[
            pltpu.VMEM((total, width), BF16),
            pltpu.VMEM((max(8, planes), count), F32),
            pltpu.VMEM((tile, width), F32),
            pltpu.VMEM((tile, 128), F32),
            pltpu.VMEM((ids.shape[0], width), F32),
            pltpu.SemaphoreType.DMA((planes,)),
        ],
        compiler_params=grant(40),
        cost_estimate=cost(4 * total * lists * width, 2 * total * width, total * lists),
        name="new_centroids",
    )(place, in_hbm(centroids), column, *rows, in_hbm(own), *halves, ids)


def residual_kernel(*refs):
    slot_ref, own_ref = refs[0:2]
    pieces = refs[2:-2]
    out_ref, table = refs[-2:]
    each = pieces[0].shape[0]
    for index, piece in enumerate(pieces):
        table[index * each : (index + 1) * each, :] = piece[...].astype(F32)
    count, slots = own_ref.shape[0], table.shape[0]
    wanted = slot_ref[...] == lax.broadcasted_iota(jnp.int32, (count, slots), 1)
    chosen = lax.dot_general(
        wanted.astype(F32).astype(BF16), table[...].astype(BF16), NN, preferred_element_type=F32
    )
    out_ref[...] = (own_ref[...].astype(F32) - chosen).astype(BF16)


def subtract_rows(slots, own, pieces):
    return pl.pallas_call(
        residual_kernel,
        out_shape=jax.ShapeDtypeStruct(own.shape, BF16),
        scratch_shapes=[pltpu.VMEM((len(pieces) * pieces[0].shape[0], own.shape[1]), F32)],
        compiler_params=grant(16),
        name="subtract_rows",
    )(slots, own, *pieces)


def swap(value, axis, key):
    count = lax.axis_size(axis)
    return lax.ppermute(value, axis, [(i, i ^ key) for i in range(count)])


def everywhere(value, axis, step=1):
    return [value] + [swap(value, axis, key) for key in range(step, lax.axis_size(axis), step)]


def after(value, *others):
    return lax.optimization_barrier((value,) + others)[0]


def step_on_device(vectors, centroids, assignment):
    row_count, _ = vectors.shape
    list_count = centroids.shape[0]
    data_count = lax.axis_size("dp")
    owner_count = lax.axis_size("cent")
    me = lax.axis_index("cent")
    place = jnp.stack([lax.axis_index("dp"), me]).astype(jnp.int32)
    send_count = row_count // owner_count
    capacity = max(2, 2 * send_count // owner_count)
    slot_count = owner_count * capacity
    ratio = row_count * data_count / (list_count * owner_count)
    log_mass = math.log(ratio)

    own = lax.dynamic_slice_in_dim(vectors, me * send_count, send_count, 0)
    keys = jnp.bitwise_xor(assignment // list_count, me)
    local_ids = assignment % list_count
    positions = jnp.arange(send_count, dtype=jnp.int32)
    earlier_same = (keys[:, None] == keys[None, :]) & (positions[None, :] < positions[:, None])
    slots = keys * capacity + jnp.sum(earlier_same.astype(jnp.int32), axis=1)
    picked = slots[:, None] == jnp.arange(row_count, dtype=jnp.int32)[None, :]
    outgoing_ids = jnp.sum(jnp.where(picked, local_ids[:, None], 0), axis=0)
    ids_row = outgoing_ids.astype(F32)[None, :]

    def across(piece, *ready):
        return everywhere(after(piece, *ready), "cent", 2)

    def partners(pieces):
        half = jnp.concatenate(pieces, axis=0)
        return [half, swap(half, "cent", 1)]

    arriving = [swap(own, "dp", 1)]
    logits, stats = logits_and_stats(vectors, centroids)
    parts = everywhere(stats, "dp")
    if data_count > 2:
        arriving.append(swap(after(own, stats), "dp", 2))
    moved = across(arriving[0], stats)
    scaled, own_stats, first_column = first_rows(logits, ids_row, parts, log_mass)
    partner = swap(own_stats, "cent", 1)
    pair = jnp.concatenate(
        join_pairs([own_stats, partner]) + (own_stats[2:3], partner[2:3]), axis=0
    )
    parts = everywhere(pair, "cent", 2)
    rows_of = [part[2 + key : 3 + key, :slot_count] for part in parts for key in range(2)]
    arrived = jnp.concatenate(
        [rows_of[key][0, key * capacity : (key + 1) * capacity] for key in range(owner_count)]
    ).astype(jnp.int32)

    peak = None
    halves = []
    for turn in range(1, ITERS):
        halves += partners(moved)
        moved = across(arriving[turn], pair)
        if turn == 1:
            sums, peak, scaled = column_sums(scaled, own_stats, parts)
        else:
            sums, scaled = column_sums(scaled, own_stats, parts, peak)
        parts = everywhere(sums, "dp")
        if turn == 1:
            for key in range(3, data_count):
                arriving.append(swap(after(own, sums), "dp", key))
        sums, column, scaled = row_sums(scaled, first_column, own_stats, peak, parts, ratio)
        partner = swap(sums, "cent", 1)
        pair = sums + partner
        parts = everywhere(pair, "cent", 2)
    halves += partners(moved)
    for turn in range(ITERS, data_count - 1):
        halves += partners(across(arriving[turn]))
    row = -(peak + jnp.log(tree(parts, jnp.add)))

    rows = everywhere(row, "dp")
    updated, *pieces = new_centroids(
        place, centroids, column, rows, vectors, halves, arrived[:, None], owner_count
    )
    pieces = [pieces[0]] + [swap(pieces[key], "cent", key) for key in range(1, owner_count)]
    residuals = subtract_rows(slots[:, None], own, pieces)
    return (updated, row.reshape(row_count), column.reshape(list_count), residuals)


def solution(mesh):
    in_specs = (P("dp", None), P("cent", None), P(("dp", "cent")))
    out_specs = (P("cent", None), P("dp"), P("cent"), P(("dp", "cent"), None))
    return jax.shard_map(
        step_on_device, mesh=mesh, in_specs=in_specs, out_specs=out_specs, check_vma=False
    )
```

profile of v0, /device:TPU:0, one launch (start us, length us, event | category | flops | bytes accessed | tf_op | source)
XLA Modules:
  0.0 244.3 jit_solution(4451019553980346742)
XLA Ops:
  0.6 11.1 %logits_stats.1 = (f32[2048,2048]{1,0:T(8,128)S(1)}, f32[2,2048]{1,0:T(2,128)S(1)}) custom-call(bf16[2048,768]{1,0:T(8,128)(2,1)} %refs_7_.1, bf16[2048,768]{1,0:T(8,128)(2,1)} %refs_1_.1), custom_call_target="tpu_custom_call" | custom-call | flops 6442450944 | bytes 16777216 | tf_op jit(solution)/shard_map/logits_stats/pallas_call | solution.py:76
  11.7 5.8 %copy-done.2 = f32[2048,2048]{1,0:T(8,128)} copy-done((f32[2048,2048]{1,0:T(8,128)}, f32[2048,2048]{1,0:T(8,128)S(1)}, u32[]{:S(2)}) %copy-start.2) | copy-done | bytes 16777240
  17.5 3.1 %collective-permute-start = (f32[2,2048]{1,0:T(2,128)S(1)}, f32[2,2048]{1,0:T(2,128)S(1)}, u32[]{:S(2)}, u32[]{:S(2)}) collective-permute-start(f32[2,2048]{1,0:T(2,128)S(1)} %get-tuple-element.33.refs_2_), channel_id=1, source_target_pairs={{0,8},{8,0},{16,24},{24,16},{1,9},{9,1},{17,25},{25,17},{2,10},{10... | collective-permute-start | bytes 49160 | tf_op jit(solution)/shard_map/ppermute | solution.py:409
  20.6 2.6 %collective-permute-start.1 = (f32[2,2048]{1,0:T(2,128)S(1)}, f32[2,2048]{1,0:T(2,128)S(1)}, u32[]{:S(2)}, u32[]{:S(2)}) collective-permute-start(f32[2,2048]{1,0:T(2,128)S(1)} %get-tuple-element.33.refs_2_), channel_id=1, source_target_pairs={{0,16},{8,24},{16,0},{24,8},{1,17},{9,25},{17,1},{25,9},{2,18},{10... | collective-permute-start | bytes 49160 | tf_op jit(solution)/shard_map/ppermute | solution.py:409
  23.7 1.6 collective-permute-done.1.refs_4_
  25.3 3.4 %collective-permute-done.2.refs_5_ = f32[2,2048]{1,0:T(2,128)S(1)} collective-permute-done((f32[2,2048]{1,0:T(2,128)S(1)}, f32[2,2048]{1,0:T(2,128)S(1)}, u32[]{:S(2)}, u32[]{:S(2)}) %collective-permute-start.2) | collective-permute-done | bytes 16416 | tf_op jit(solution)/shard_map/ppermute | solution.py:409
  28.7 5.8 %copy-done.3 = f32[2048,2048]{1,0:T(8,128)S(1)} copy-done((f32[2048,2048]{1,0:T(8,128)S(1)}, f32[2048,2048]{1,0:T(8,128)}, u32[]{:S(2)}) %copy-start.3) | copy-done | bytes 16777240
  34.4 8.6 %first_rows.1 = (bf16[2048,2048]{1,0:T(8,128)(2,1)S(1)}, f32[3,2048]{1,0:T(4,128)S(1)}, f32[1,2048]{1,0:T(1,128)S(1)}) custom-call(f32[2048,2048]{1,0:T(8,128)S(1)} %copy-done.3, f32[1,2048]{1,0:T(1,128)S(1)} %bitcast.22, f32[2,2048]{1,0:T(2,128)S(1)} %get-tuple-element.33.refs_2_, f32[2,2048]{1,0:T(2,128)S(1)} %collective-permute-done.refs_3_, ...), custom_call_target="tpu_custom_call" | custom-call | flops 16777216 | bytes 25165824 | tf_op jit(solution)/shard_map/first_rows/pallas_call | solution.py:125
  43.1 1.0 constant_dynamic-slice_fusion.refs_1_
  44.3 0.7 collective-permute-start.29
  45.1 2.6 %collective-permute-start.6 = (f32[4,2048]{1,0:T(4,128)S(1)}, f32[4,2048]{1,0:T(4,128)S(1)}, u32[]{:S(2)}, u32[]{:S(2)}) collective-permute-start(f32[4,2048]{1,0:T(4,128)S(1)} %pad_maximum_fusion.refs_2_), channel_id=1, source_target_pairs={{0,6},{1,7},{2,4},{3,5},{4,2},{5,3},{6,0},{7,1},{8,14},{9,15},{10,... | collective-permute-start | bytes 98312 | tf_op jit(solution)/shard_map/ppermute | solution.py:409
  48.6 1.3 collective-permute-done.6.refs_5_
  50.0 1.6 collective-permute-done.5.refs_4_
  52.1 2.3 column_sums.2
  54.4 1.3 collective-permute-start.7
  55.7 2.9 %collective-permute-start.8 = (f32[1,2048]{1,0:T(1,128)S(1)}, f32[1,2048]{1,0:T(1,128)S(1)}, u32[]{:S(2)}, u32[]{:S(2)}) collective-permute-start(f32[1,2048]{1,0:T(1,128)S(1)} %get-tuple-element.39.refs_4_), channel_id=1, source_target_pairs={{0,16},{8,24},{16,0},{24,8},{1,17},{9,25},{17,1},{25,9},{2,18},{10... | collective-permute-start | bytes 24584 | tf_op jit(solution)/shard_map/ppermute | solution.py:409
  58.8 3.6 %collective-permute-done.7.refs_5_ = f32[1,2048]{1,0:T(1,128)S(1)} collective-permute-done((f32[1,2048]{1,0:T(1,128)S(1)}, f32[1,2048]{1,0:T(1,128)S(1)}, u32[]{:S(2)}, u32[]{:S(2)}) %collective-permute-start.7) | collective-permute-done | bytes 8224 | tf_op jit(solution)/shard_map/ppermute | solution.py:409
  62.4 1.9 collective-permute-start.34
  64.3 1.5 collective-permute-done.8.refs_6_
  65.8 3.2 %row_sums.2 = (f32[1,2048]{1,0:T(1,128)S(1)}, f32[1,2048]{1,0:T(1,128)}, bf16[2048,2048]{1,0:T(8,128)(2,1)S(1)}) custom-call(bf16[2048,2048]{1,0:T(8,128)(2,1)S(1)} %get-tuple-element.36.refs_0_, f32[1,2048]{1,0:T(1,128)S(1)} %get-tuple-element.37.refs_1_, f32[3,2048]{1,0:T(4,128)S(1)} %get-tuple-element.35.refs_1_.refs_2_, ...), custom_call_target="tpu_custom_call", output_to_operand_aliasing={{2}: (0, {})} | custom-call | flops 67108864 | bytes 8388608 | tf_op jit(solution)/shard_map/row_sums/pallas_call | solution.py:232
  69.0 3.3 %copy-done = bf16[2048,2048]{1,0:T(8,128)(2,1)} copy-done((bf16[2048,2048]{1,0:T(8,128)(2,1)}, bf16[2048,2048]{1,0:T(8,128)(2,1)S(1)}, u32[]{:S(2)}) %copy-start) | copy-done | bytes 8388632
  72.3 1.2 collective-permute-done.10
  73.5 1.6 collective-permute-start.11
  75.0 1.5 collective-permute-start.12
  77.2 1.5 collective-permute-start.30
  78.8 2.4 collective-permute-done.13.refs_5_
  81.2 3.4 %copy-done.1 = bf16[2048,2048]{1,0:T(8,128)(2,1)S(1)} copy-done((bf16[2048,2048]{1,0:T(8,128)(2,1)S(1)}, bf16[2048,2048]{1,0:T(8,128)(2,1)}, u32[]{:S(2)}) %copy-start.1) | copy-done | bytes 8388632
  84.6 2.3 column_sums.3
  86.9 0.6 collective-permute-start.14
  88.0 1.8 constant_dynamic-update-slice_fusion.7
  89.8 1.4 collective-permute-start.32
  91.2 0.8 constant_dynamic-update-slice_fusion.3
  92.0 1.6 collective-permute-start.25
  94.2 0.8 constant_dynamic-update-slice_fusion.6
  95.0 15.8 %collective-permute-done.31 = bf16[256,768]{1,0:T(8,128)(2,1)S(1)} collective-permute-done((bf16[256,768]{1,0:T(8,128)(2,1)}, bf16[256,768]{1,0:T(8,128)(2,1)S(1)}, u32[]{:S(2)}, u32[]{:S(2)}) %collective-permute-start.31) | collective-permute-done | bytes 393248 | tf_op jit(solution)/shard_map/ppermute | solution.py:409
  110.8 0.8 constant_dynamic-update-slice_fusion.5
  111.7 1.3 collective-permute-start.35
  112.9 0.8 constant_dynamic-update-slice_fusion.4.refs_10_
  113.8 2.2 collective-permute-start.36
  116.0 0.8 constant_dynamic-update-slice_fusion.2
  116.8 12.4 %collective-permute-done.26 = bf16[256,768]{1,0:T(8,128)(2,1)S(1)} collective-permute-done((bf16[256,768]{1,0:T(8,128)(2,1)S(1)}, bf16[256,768]{1,0:T(8,128)(2,1)S(1)}, u32[]{:S(2)}, u32[]{:S(2)}) %collective-permute-start.26) | collective-permute-done | bytes 393248 | tf_op jit(solution)/shard_map/ppermute | solution.py:409
  129.6 0.8 constant_dynamic-update-slice_fusion.1
  130.4 1.3 collective-permute-start.15
  131.7 0.8 constant_dynamic-update-slice_fusion.refs_8_
  132.5 2.4 collective-permute-start.16
  135.0 4.0 %collective-permute-done.36 = bf16[256,768]{1,0:T(8,128)(2,1)S(1)} collective-permute-done((bf16[256,768]{1,0:T(8,128)(2,1)S(1)}, bf16[256,768]{1,0:T(8,128)(2,1)S(1)}, u32[]{:S(2)}, u32[]{:S(2)}) %collective-permute-start.36) | collective-permute-done | bytes 393248 | tf_op jit(solution)/shard_map/ppermute | solution.py:409
  139.7 3.2 %row_sums.3 = (f32[1,2048]{1,0:T(1,128)S(1)}, f32[1,2048]{1,0:T(1,128)}, bf16[2048,2048]{1,0:T(8,128)(2,1)S(1)}) custom-call(bf16[2048,2048]{1,0:T(8,128)(2,1)S(1)} %get-tuple-element.42.refs_0_, f32[1,2048]{1,0:T(1,128)S(1)} %get-tuple-element.37.refs_1_, f32[3,2048]{1,0:T(4,128)S(1)} %get-tuple-element.35.refs_1_.refs_2_, ...), custom_call_target="tpu_custom_call", output_to_operand_aliasing={{2}: (0, {})} | custom-call | flops 67108864 | bytes 8388608 | tf_op jit(solution)/shard_map/row_sums/pallas_call | solution.py:232
  143.4 3.9 %collective-permute-done.17 = f32[1,2048]{1,0:T(1,128)S(1)} collective-permute-done((f32[1,2048]{1,0:T(1,128)S(1)}, f32[1,2048]{1,0:T(1,128)S(1)}, u32[]{:S(2)}, u32[]{:S(2)}) %collective-permute-start.17) | collective-permute-done | bytes 8224 | tf_op jit(solution)/shard_map/ppermute | solution.py:409
  148.5 2.5 %collective-permute-done.18 = f32[1,2048]{1,0:T(1,128)S(1)} collective-permute-done((f32[1,2048]{1,0:T(1,128)S(1)}, f32[1,2048]{1,0:T(1,128)S(1)}, u32[]{:S(2)}, u32[]{:S(2)}) %collective-permute-start.18) | collective-permute-done | bytes 8224 | tf_op jit(solution)/shard_map/ppermute | solution.py:409
  151.6 3.9 %collective-permute-done.20 = f32[1,2048]{1,0:T(1,128)S(1)} collective-permute-done((f32[1,2048]{1,0:T(1,128)S(1)}, f32[1,2048]{1,0:T(1,128)S(1)}, u32[]{:S(2)}, u32[]{:S(2)}) %collective-permute-start.20) | collective-permute-done | bytes 8224 | tf_op jit(solution)/shard_map/ppermute | solution.py:409
  155.6 1.5 collective-permute-start.21
  157.6 1.6 collective-permute-done.21.refs_4_
  159.3 1.4 collective-permute-start.23
  161.0 0.7 collective-permute-done.22.refs_5_
  161.7 3.1 %collective-permute-done.23.refs_6_ = f32[1,2048]{1,0:T(1,128)S(1)} collective-permute-done((f32[1,2048]{1,0:T(1,128)S(1)}, f32[1,2048]{1,0:T(1,128)S(1)}, u32[]{:S(2)}, u32[]{:S(2)}) %collective-permute-start.23) | collective-permute-done | bytes 8224 | tf_op jit(solution)/shard_map/ppermute | solution.py:409
  164.7 0.7 copy-done.5
  165.4 65.0 %new_centroids.1 = (bf16[2048,768]{1,0:T(8,128)(2,1)}, bf16[64,768]{1,0:T(8,128)(2,1)S(1)}, bf16[64,768]{1,0:T(8,128)(2,1)S(1)}, bf16[64,768]{1,0:T(8,128)(2,1)S...) custom-call(s32[2]{0:T(128)S(1)} %pad_add_fusion.refs_0_, ...), custom_call_target="tpu_custom_call" | custom-call | flops 51539607552 | bytes 12582912 | tf_op jit(solution)/shard_map/new_centroids/pallas_call | solution.py:353
  230.5 0.6 collective-permute-start.40
  231.1 1.2 collective-permute-start.41
  232.9 1.2 collective-permute-start.43
  234.6 1.6 collective-permute-done.40.refs_4_
  237.3 0.8 collective-permute-done.42.refs_6_
  238.1 5.1 %collective-permute-done.43.refs_7_ = bf16[64,768]{1,0:T(8,128)(2,1)S(1)} collective-permute-done((bf16[64,768]{1,0:T(8,128)(2,1)S(1)}, bf16[64,768]{1,0:T(8,128)(2,1)S(1)}, u32[]{:S(2)}, u32[]{:S(2)}) %collective-permute-start.43) | collective-permute-done | bytes 98336 | tf_op jit(solution)/shard_map/ppermute | solution.py:409
  243.2 1.2 subtract_rows.1
  (83 shorter events, 10.9 us)
Async XLA Ops:
  0.6 22.5 %copy-start.6 = (s32[256]{0:T(256)S(1)}, s32[256]{0:T(256)}, u32[]{:S(2)}) copy-start(s32[256]{0:T(256)} %param.5) | copy-start | bytes 3076
  11.7 5.8 %copy-start.2 = (f32[2048,2048]{1,0:T(8,128)}, f32[2048,2048]{1,0:T(8,128)S(1)}, u32[]{:S(2)}) copy-start(f32[2048,2048]{1,0:T(8,128)S(1)} %get-tuple-element.32.refs_0_) | copy-start | bytes 50331652
  17.5 6.2 %collective-permute-start = (f32[2,2048]{1,0:T(2,128)S(1)}, f32[2,2048]{1,0:T(2,128)S(1)}, u32[]{:S(2)}, u32[]{:S(2)}) collective-permute-start(f32[2,2048]{1,0:T(2,128)S(1)} %get-tuple-element.33.refs_2_), channel_id=1, source_target_pairs={{0,8},{8,0},{16,24},{24,16},{1,9},{9,1},{17,25},{25,17},{2,10},{10... | collective-permute-start | bytes 49160 | tf_op jit(solution)/shard_map/ppermute | solution.py:409
  20.6 4.7 %collective-permute-start.1 = (f32[2,2048]{1,0:T(2,128)S(1)}, f32[2,2048]{1,0:T(2,128)S(1)}, u32[]{:S(2)}, u32[]{:S(2)}) collective-permute-start(f32[2,2048]{1,0:T(2,128)S(1)} %get-tuple-element.33.refs_2_), channel_id=1, source_target_pairs={{0,16},{8,24},{16,0},{24,8},{1,17},{9,25},{17,1},{25,9},{2,18},{10... | collective-permute-start | bytes 49160 | tf_op jit(solution)/shard_map/ppermute | solution.py:409
  23.1 5.5 %collective-permute-start.2 = (f32[2,2048]{1,0:T(2,128)S(1)}, f32[2,2048]{1,0:T(2,128)S(1)}, u32[]{:S(2)}, u32[]{:S(2)}) collective-permute-start(f32[2,2048]{1,0:T(2,128)S(1)} %get-tuple-element.33.refs_2_), channel_id=1, source_target_pairs={{0,24},{8,16},{16,8},{24,0},{1,25},{9,17},{17,9},{25,1},{2,26},{10... | collective-permute-start | bytes 49160 | tf_op jit(solution)/shard_map/ppermute | solution.py:409
  28.7 5.8 %copy-start.3 = (f32[2048,2048]{1,0:T(8,128)S(1)}, f32[2048,2048]{1,0:T(8,128)}, u32[]{:S(2)}) copy-start(f32[2048,2048]{1,0:T(8,128)} %copy-done.2) | copy-start | bytes 50331652
  43.1 1.9 collective-permute-start.3
  44.2 45.7 %collective-permute-start.24 = (bf16[256,768]{1,0:T(8,128)(2,1)S(1)}, bf16[256,768]{1,0:T(8,128)(2,1)S(1)}, u32[]{:S(2)}, u32[]{:S(2)}) collective-permute-start(bf16[256,768]{1,0:T(8,128)(2,1)S(1)} %constant_dynamic-slice_fusion.refs_1_), channel_id=1, source_target_pairs={{0,8},{8,0},{16,24},{24,16},{1,9},{9,1},{17,25},{25,17},{2,10},{10... | collective-permute-start | bytes 1179656 | tf_op jit(solution)/shard_map/ppermute | solution.py:409
  44.3 32.3 %collective-permute-start.29 = (bf16[256,768]{1,0:T(8,128)(2,1)S(1)}, bf16[256,768]{1,0:T(8,128)(2,1)}, u32[]{:S(2)}, u32[]{:S(2)}) collective-permute-start(bf16[256,768]{1,0:T(8,128)(2,1)S(1)} %constant_dynamic-slice_fusion.refs_1_), channel_id=1, source_target_pairs={{0,16},{8,24},{16,0},{24,8},{1,17},{9,25},{17,1},{25,9},{2,18},{10... | collective-permute-start | bytes 1179656 | tf_op jit(solution)/shard_map/ppermute | solution.py:409
  45.1 4.9 %collective-permute-start.6 = (f32[4,2048]{1,0:T(4,128)S(1)}, f32[4,2048]{1,0:T(4,128)S(1)}, u32[]{:S(2)}, u32[]{:S(2)}) collective-permute-start(f32[4,2048]{1,0:T(4,128)S(1)} %pad_maximum_fusion.refs_2_), channel_id=1, source_target_pairs={{0,6},{1,7},{2,4},{3,5},{4,2},{5,3},{6,0},{7,1},{8,14},{9,15},{10,... | collective-permute-start | bytes 98312 | tf_op jit(solution)/shard_map/ppermute | solution.py:409
  47.6 3.9 %collective-permute-start.5 = (f32[4,2048]{1,0:T(4,128)S(1)}, f32[4,2048]{1,0:T(4,128)S(1)}, u32[]{:S(2)}, u32[]{:S(2)}) collective-permute-start(f32[4,2048]{1,0:T(4,128)S(1)} %pad_maximum_fusion.refs_2_), channel_id=1, source_target_pairs={{0,4},{1,5},{2,6},{3,7},{4,0},{5,1},{6,2},{7,3},{8,12},{9,13},{10,... | collective-permute-start | bytes 98312 | tf_op jit(solution)/shard_map/ppermute | solution.py:409
  48.1 3.9 %collective-permute-start.4 = (f32[4,2048]{1,0:T(4,128)S(1)}, f32[4,2048]{1,0:T(4,128)S(1)}, u32[]{:S(2)}, u32[]{:S(2)}) collective-permute-start(f32[4,2048]{1,0:T(4,128)S(1)} %pad_maximum_fusion.refs_2_), channel_id=1, source_target_pairs={{0,2},{1,3},{2,0},{3,1},{4,6},{5,7},{6,4},{7,5},{8,10},{9,11},{10,... | collective-permute-start | bytes 98312 | tf_op jit(solution)/shard_map/ppermute | solution.py:409
  54.4 8.0 %collective-permute-start.7 = (f32[1,2048]{1,0:T(1,128)S(1)}, f32[1,2048]{1,0:T(1,128)S(1)}, u32[]{:S(2)}, u32[]{:S(2)}) collective-permute-start(f32[1,2048]{1,0:T(1,128)S(1)} %get-tuple-element.39.refs_4_), channel_id=1, source_target_pairs={{0,8},{8,0},{16,24},{24,16},{1,9},{9,1},{17,25},{25,17},{2,10},{10... | collective-permute-start | bytes 24584 | tf_op jit(solution)/shard_map/ppermute | solution.py:409
  55.7 10.2 %collective-permute-start.8 = (f32[1,2048]{1,0:T(1,128)S(1)}, f32[1,2048]{1,0:T(1,128)S(1)}, u32[]{:S(2)}, u32[]{:S(2)}) collective-permute-start(f32[1,2048]{1,0:T(1,128)S(1)} %get-tuple-element.39.refs_4_), channel_id=1, source_target_pairs={{0,16},{8,24},{16,0},{24,8},{1,17},{9,25},{17,1},{25,9},{2,18},{10... | collective-permute-start | bytes 24584 | tf_op jit(solution)/shard_map/ppermute | solution.py:409
  58.6 7.3 %collective-permute-start.9 = (f32[1,2048]{1,0:T(1,128)S(1)}, f32[1,2048]{1,0:T(1,128)S(1)}, u32[]{:S(2)}, u32[]{:S(2)}) collective-permute-start(f32[1,2048]{1,0:T(1,128)S(1)} %get-tuple-element.39.refs_4_), channel_id=1, source_target_pairs={{0,24},{8,16},{16,8},{24,0},{1,25},{9,17},{17,9},{25,1},{2,26},{10... | collective-permute-start | bytes 24584 | tf_op jit(solution)/shard_map/ppermute | solution.py:409
  62.4 29.6 %collective-permute-start.34 = (bf16[256,768]{1,0:T(8,128)(2,1)S(1)}, bf16[256,768]{1,0:T(8,128)(2,1)S(1)}, u32[]{:S(2)}, u32[]{:S(2)}) collective-permute-start(bf16[256,768]{1,0:T(8,128)(2,1)S(1)} %constant_dynamic-slice_fusion.refs_1_), channel_id=1, source_target_pairs={{0,24},{8,16},{16,8},{24,0},{1,25},{9,17},{17,9},{25,1},{2,26},{10... | collective-permute-start | bytes 1179656 | tf_op jit(solution)/shard_map/ppermute | solution.py:409
  69.0 3.3 %copy-start = (bf16[2048,2048]{1,0:T(8,128)(2,1)}, bf16[2048,2048]{1,0:T(8,128)(2,1)S(1)}, u32[]{:S(2)}) copy-start(bf16[2048,2048]{1,0:T(8,128)(2,1)S(1)} %get-tuple-element.40.refs_0_) | copy-start | bytes 25165828
  72.3 1.2 collective-permute-start.10
  73.5 3.7 %collective-permute-start.11 = (f32[1,2048]{1,0:T(1,128)S(1)}, f32[1,2048]{1,0:T(1,128)S(1)}, u32[]{:S(2)}, u32[]{:S(2)}) collective-permute-start(f32[1,2048]{1,0:T(1,128)S(1)} %add.37.refs_2_), channel_id=1, source_target_pairs={{0,2},{1,3},{2,0},{3,1},{4,6},{5,7},{6,4},{7,5},{8,10},{9,11},{10,... | collective-permute-start | bytes 24584 | tf_op jit(solution)/shard_map/ppermute | solution.py:409
  75.0 3.7 %collective-permute-start.12 = (f32[1,2048]{1,0:T(1,128)S(1)}, f32[1,2048]{1,0:T(1,128)S(1)}, u32[]{:S(2)}, u32[]{:S(2)}) collective-permute-start(f32[1,2048]{1,0:T(1,128)S(1)} %add.37.refs_2_), channel_id=1, source_target_pairs={{0,4},{1,5},{2,6},{3,7},{4,0},{5,1},{6,2},{7,3},{8,12},{9,13},{10,... | collective-permute-start | bytes 24584 | tf_op jit(solution)/shard_map/ppermute | solution.py:409
  76.6 4.6 %collective-permute-start.13 = (f32[1,2048]{1,0:T(1,128)S(1)}, f32[1,2048]{1,0:T(1,128)S(1)}, u32[]{:S(2)}, u32[]{:S(2)}) collective-permute-start(f32[1,2048]{1,0:T(1,128)S(1)} %add.37.refs_2_), channel_id=1, source_target_pairs={{0,6},{1,7},{2,4},{3,5},{4,2},{5,3},{6,0},{7,1},{8,14},{9,15},{10,... | collective-permute-start | bytes 24584 | tf_op jit(solution)/shard_map/ppermute | solution.py:409
  77.2 16.4 %collective-permute-start.30 = (bf16[256,768]{1,0:T(8,128)(2,1)}, bf16[256,768]{1,0:T(8,128)(2,1)S(1)}, u32[]{:S(2)}, u32[]{:S(2)}) collective-permute-start(bf16[256,768]{1,0:T(8,128)(2,1)} %collective-permute-done.29), channel_id=1, source_target_pairs={{0,2},{1,3},{2,0},{3,1},{4,6},{5,7},{6,4},{7,5},{8,10},{9,11},{10,... | collective-permute-start | bytes 1179656 | tf_op jit(solution)/shard_map/ppermute | solution.py:409
  81.2 3.4 %copy-start.1 = (bf16[2048,2048]{1,0:T(8,128)(2,1)S(1)}, bf16[2048,2048]{1,0:T(8,128)(2,1)}, u32[]{:S(2)}) copy-start(bf16[2048,2048]{1,0:T(8,128)(2,1)} %copy-done) | copy-start | bytes 25165828
  86.9 52.7 %collective-permute-start.14 = (f32[1,2048]{1,0:T(1,128)S(1)}, f32[1,2048]{1,0:T(1,128)S(1)}, u32[]{:S(2)}, u32[]{:S(2)}) collective-permute-start(f32[1,2048]{1,0:T(1,128)S(1)} %get-tuple-element.43.refs_4_), channel_id=1, source_target_pairs={{0,8},{8,0},{16,24},{24,16},{1,9},{9,1},{17,25},{25,17},{2,10},{10... | collective-permute-start | bytes 24584 | tf_op jit(solution)/shard_map/ppermute | solution.py:409
  87.5 23.3 %collective-permute-start.31 = (bf16[256,768]{1,0:T(8,128)(2,1)}, bf16[256,768]{1,0:T(8,128)(2,1)S(1)}, u32[]{:S(2)}, u32[]{:S(2)}) collective-permute-start(bf16[256,768]{1,0:T(8,128)(2,1)} %collective-permute-done.29), channel_id=1, source_target_pairs={{0,4},{1,5},{2,6},{3,7},{4,0},{5,1},{6,2},{7,3},{8,12},{9,13},{10,... | collective-permute-start | bytes 1179656 | tf_op jit(solution)/shard_map/ppermute | solution.py:409
  89.8 21.8 %collective-permute-start.32 = (bf16[256,768]{1,0:T(8,128)(2,1)}, bf16[256,768]{1,0:T(8,128)(2,1)S(1)}, u32[]{:S(2)}, u32[]{:S(2)}) collective-permute-start(bf16[256,768]{1,0:T(8,128)(2,1)} %collective-permute-done.29), channel_id=1, source_target_pairs={{0,6},{1,7},{2,4},{3,5},{4,2},{5,3},{6,0},{7,1},{8,14},{9,15},{10,... | collective-permute-start | bytes 1179656 | tf_op jit(solution)/shard_map/ppermute | solution.py:409
  92.0 21.7 %collective-permute-start.25 = (bf16[256,768]{1,0:T(8,128)(2,1)S(1)}, bf16[256,768]{1,0:T(8,128)(2,1)S(1)}, u32[]{:S(2)}, u32[]{:S(2)}) collective-permute-start(bf16[256,768]{1,0:T(8,128)(2,1)S(1)} %collective-permute-done.24), channel_id=1, source_target_pairs={{0,2},{1,3},{2,0},{3,1},{4,6},{5,7},{6,4},{7,5},{8,10},{9,11},{10,... | collective-permute-start | bytes 1179656 | tf_op jit(solution)/shard_map/ppermute | solution.py:409
  93.6 35.6 %collective-permute-start.26 = (bf16[256,768]{1,0:T(8,128)(2,1)S(1)}, bf16[256,768]{1,0:T(8,128)(2,1)S(1)}, u32[]{:S(2)}, u32[]{:S(2)}) collective-permute-start(bf16[256,768]{1,0:T(8,128)(2,1)S(1)} %collective-permute-done.24), channel_id=1, source_target_pairs={{0,4},{1,5},{2,6},{3,7},{4,0},{5,1},{6,2},{7,3},{8,12},{9,13},{10,... | collective-permute-start | bytes 1179656 | tf_op jit(solution)/shard_map/ppermute | solution.py:409
  110.8 19.5 %collective-permute-start.27 = (bf16[256,768]{1,0:T(8,128)(2,1)S(1)}, bf16[256,768]{1,0:T(8,128)(2,1)S(1)}, u32[]{:S(2)}, u32[]{:S(2)}) collective-permute-start(bf16[256,768]{1,0:T(8,128)(2,1)S(1)} %collective-permute-done.24), channel_id=1, source_target_pairs={{0,6},{1,7},{2,4},{3,5},{4,2},{5,3},{6,0},{7,1},{8,14},{9,15},{10,... | collective-permute-start | bytes 1179656 | tf_op jit(solution)/shard_map/ppermute | solution.py:409
  111.7 20.8 %collective-permute-start.35 = (bf16[256,768]{1,0:T(8,128)(2,1)S(1)}, bf16[256,768]{1,0:T(8,128)(2,1)S(1)}, u32[]{:S(2)}, u32[]{:S(2)}) collective-permute-start(bf16[256,768]{1,0:T(8,128)(2,1)S(1)} %collective-permute-done.34), channel_id=1, source_target_pairs={{0,2},{1,3},{2,0},{3,1},{4,6},{5,7},{6,4},{7,5},{8,10},{9,11},{10,... | collective-permute-start | bytes 1179656 | tf_op jit(solution)/shard_map/ppermute | solution.py:409
  113.8 25.2 %collective-permute-start.36 = (bf16[256,768]{1,0:T(8,128)(2,1)S(1)}, bf16[256,768]{1,0:T(8,128)(2,1)S(1)}, u32[]{:S(2)}, u32[]{:S(2)}) collective-permute-start(bf16[256,768]{1,0:T(8,128)(2,1)S(1)} %collective-permute-done.34), channel_id=1, source_target_pairs={{0,4},{1,5},{2,6},{3,7},{4,0},{5,1},{6,2},{7,3},{8,12},{9,13},{10,... | collective-permute-start | bytes 1179656 | tf_op jit(solution)/shard_map/ppermute | solution.py:409
  129.2 9.8 %collective-permute-start.37 = (bf16[256,768]{1,0:T(8,128)(2,1)S(1)}, bf16[256,768]{1,0:T(8,128)(2,1)S(1)}, u32[]{:S(2)}, u32[]{:S(2)}) collective-permute-start(bf16[256,768]{1,0:T(8,128)(2,1)S(1)} %collective-permute-done.34), channel_id=1, source_target_pairs={{0,6},{1,7},{2,4},{3,5},{4,2},{5,3},{6,0},{7,1},{8,14},{9,15},{10,... | collective-permute-start | bytes 1179656 | tf_op jit(solution)/shard_map/ppermute | solution.py:409
  130.4 9.3 %collective-permute-start.15 = (f32[1,2048]{1,0:T(1,128)S(1)}, f32[1,2048]{1,0:T(1,128)S(1)}, u32[]{:S(2)}, u32[]{:S(2)}) collective-permute-start(f32[1,2048]{1,0:T(1,128)S(1)} %get-tuple-element.43.refs_4_), channel_id=1, source_target_pairs={{0,16},{8,24},{16,0},{24,8},{1,17},{9,25},{17,1},{25,9},{2,18},{10... | collective-permute-start | bytes 24584 | tf_op jit(solution)/shard_map/ppermute | solution.py:409
  132.5 7.2 %collective-permute-start.16 = (f32[1,2048]{1,0:T(1,128)S(1)}, f32[1,2048]{1,0:T(1,128)S(1)}, u32[]{:S(2)}, u32[]{:S(2)}) collective-permute-start(f32[1,2048]{1,0:T(1,128)S(1)} %get-tuple-element.43.refs_4_), channel_id=1, source_target_pairs={{0,24},{8,16},{16,8},{24,0},{1,25},{9,17},{17,9},{25,1},{2,26},{10... | collective-permute-start | bytes 24584 | tf_op jit(solution)/shard_map/ppermute | solution.py:409
  139.0 25.7 %collective-permute-start.33 = (bf16[1024,768]{1,0:T(8,128)(2,1)}, bf16[1024,768]{1,0:T(8,128)(2,1)}, u32[]{:S(2)}, u32[]{:S(2)}) collective-permute-start(bf16[1024,768]{1,0:T(8,128)(2,1)} %constant_dynamic-update-slice_fusion.4.refs_10_), channel_id=1, source_target_pairs={{0,1},{1,0},{2,3},{3,2},{4,5},{5,4},{6,7},{7,6},{8,9},{9,8},{10,11... | collective-permute-start | bytes 4718600 | tf_op jit(solution)/shard_map/ppermute | solution.py:409
  139.0 25.7 %collective-permute-start.28 = (bf16[1024,768]{1,0:T(8,128)(2,1)}, bf16[1024,768]{1,0:T(8,128)(2,1)}, u32[]{:S(2)}, u32[]{:S(2)}) collective-permute-start(bf16[1024,768]{1,0:T(8,128)(2,1)} %constant_dynamic-update-slice_fusion.refs_8_), channel_id=1, source_target_pairs={{0,1},{1,0},{2,3},{3,2},{4,5},{5,4},{6,7},{7,6},{8,9},{9,8},{10,11... | collective-permute-start | bytes 4718600 | tf_op jit(solution)/shard_map/ppermute | solution.py:409
  139.6 25.1 %collective-permute-start.38 = (bf16[1024,768]{1,0:T(8,128)(2,1)S(1)}, bf16[1024,768]{1,0:T(8,128)(2,1)}, u32[]{:S(2)}, u32[]{:S(2)}) collective-permute-start(bf16[1024,768]{1,0:T(8,128)(2,1)S(1)} %constant_dynamic-update-slice_fusion.8.refs_12_), channel_id=1, source_target_pairs={{0,1},{1,0},{2,3},{3,2},{4,5},{5,4},{6,7},{7,6},{8,9},{9,8},{10,11... | collective-permute-start | bytes 4718600 | tf_op jit(solution)/shard_map/ppermute | solution.py:409
  142.9 4.3 %collective-permute-start.17 = (f32[1,2048]{1,0:T(1,128)S(1)}, f32[1,2048]{1,0:T(1,128)S(1)}, u32[]{:S(2)}, u32[]{:S(2)}) collective-permute-start(f32[1,2048]{1,0:T(1,128)S(1)} %get-tuple-element.45), channel_id=1, source_target_pairs={{0,1},{1,0},{2,3},{3,2},{4,5},{5,4},{6,7},{7,6},{8,9},{9,8},{10,11... | collective-permute-start | bytes 24584 | tf_op jit(solution)/shard_map/ppermute | solution.py:409
  147.2 3.7 %collective-permute-start.18 = (f32[1,2048]{1,0:T(1,128)S(1)}, f32[1,2048]{1,0:T(1,128)S(1)}, u32[]{:S(2)}, u32[]{:S(2)}) collective-permute-start(f32[1,2048]{1,0:T(1,128)S(1)} %add.38), channel_id=1, source_target_pairs={{0,2},{1,3},{2,0},{3,1},{4,6},{5,7},{6,4},{7,5},{8,10},{9,11},{10,... | collective-permute-start | bytes 24584 | tf_op jit(solution)/shard_map/ppermute | solution.py:409
  147.9 3.7 %collective-permute-start.19 = (f32[1,2048]{1,0:T(1,128)S(1)}, f32[1,2048]{1,0:T(1,128)S(1)}, u32[]{:S(2)}, u32[]{:S(2)}) collective-permute-start(f32[1,2048]{1,0:T(1,128)S(1)} %add.38), channel_id=1, source_target_pairs={{0,4},{1,5},{2,6},{3,7},{4,0},{5,1},{6,2},{7,3},{8,12},{9,13},{10,... | collective-permute-start | bytes 24584 | tf_op jit(solution)/shard_map/ppermute | solution.py:409
  151.0 4.5 %collective-permute-start.20 = (f32[1,2048]{1,0:T(1,128)S(1)}, f32[1,2048]{1,0:T(1,128)S(1)}, u32[]{:S(2)}, u32[]{:S(2)}) collective-permute-start(f32[1,2048]{1,0:T(1,128)S(1)} %add.38), channel_id=1, source_target_pairs={{0,6},{1,7},{2,4},{3,5},{4,2},{5,3},{6,0},{7,1},{8,14},{9,15},{10,... | collective-permute-start | bytes 24584 | tf_op jit(solution)/shard_map/ppermute | solution.py:409
  155.5 74.9 %copy-start.4 = (f32[1,2048]{1,0:T(1,128)}, f32[1,2048]{1,0:T(1,128)S(1)}, u32[]{:S(2)}) copy-start(f32[1,2048]{1,0:T(1,128)S(1)} %add_negate_fusion.refs_3_) | copy-start | bytes 24580
  155.6 3.7 %collective-permute-start.21 = (f32[1,2048]{1,0:T(1,128)S(1)}, f32[1,2048]{1,0:T(1,128)S(1)}, u32[]{:S(2)}, u32[]{:S(2)}) collective-permute-start(f32[1,2048]{1,0:T(1,128)S(1)} %add_negate_fusion.refs_3_), channel_id=1, source_target_pairs={{0,8},{8,0},{16,24},{24,16},{1,9},{9,1},{17,25},{25,17},{2,10},{10... | collective-permute-start | bytes 24584 | tf_op jit(solution)/shard_map/ppermute | solution.py:409
  157.1 4.6 %collective-permute-start.22 = (f32[1,2048]{1,0:T(1,128)S(1)}, f32[1,2048]{1,0:T(1,128)S(1)}, u32[]{:S(2)}, u32[]{:S(2)}) collective-permute-start(f32[1,2048]{1,0:T(1,128)S(1)} %add_negate_fusion.refs_3_), channel_id=1, source_target_pairs={{0,16},{8,24},{16,0},{24,8},{1,17},{9,25},{17,1},{25,9},{2,18},{10... | collective-permute-start | bytes 24584 | tf_op jit(solution)/shard_map/ppermute | solution.py:409
  159.3 5.4 %collective-permute-start.23 = (f32[1,2048]{1,0:T(1,128)S(1)}, f32[1,2048]{1,0:T(1,128)S(1)}, u32[]{:S(2)}, u32[]{:S(2)}) collective-permute-start(f32[1,2048]{1,0:T(1,128)S(1)} %add_negate_fusion.refs_3_), channel_id=1, source_target_pairs={{0,24},{8,16},{16,8},{24,0},{1,25},{9,17},{17,9},{25,1},{2,26},{10... | collective-permute-start | bytes 24584 | tf_op jit(solution)/shard_map/ppermute | solution.py:409
  164.7 0.7 copy-start.5
  230.5 3.6 %collective-permute-start.39 = (bf16[64,768]{1,0:T(8,128)(2,1)S(1)}, bf16[64,768]{1,0:T(8,128)(2,1)S(1)}, u32[]{:S(2)}, u32[]{:S(2)}) collective-permute-start(bf16[64,768]{1,0:T(8,128)(2,1)S(1)} %get-tuple-element.53), channel_id=1, source_target_pairs={{0,1},{1,0},{2,3},{3,2},{4,5},{5,4},{6,7},{7,6},{8,9},{9,8},{10,11... | collective-permute-start | bytes 294920 | tf_op jit(solution)/shard_map/ppermute | solution.py:409
  230.5 5.7 %collective-permute-start.40 = (bf16[64,768]{1,0:T(8,128)(2,1)S(1)}, bf16[64,768]{1,0:T(8,128)(2,1)S(1)}, u32[]{:S(2)}, u32[]{:S(2)}) collective-permute-start(bf16[64,768]{1,0:T(8,128)(2,1)S(1)} %get-tuple-element.54), channel_id=1, source_target_pairs={{0,2},{1,3},{2,0},{3,1},{4,6},{5,7},{6,4},{7,5},{8,10},{9,11},{10,... | collective-permute-start | bytes 294920 | tf_op jit(solution)/shard_map/ppermute | solution.py:409
  231.1 6.2 %collective-permute-start.41 = (bf16[64,768]{1,0:T(8,128)(2,1)S(1)}, bf16[64,768]{1,0:T(8,128)(2,1)S(1)}, u32[]{:S(2)}, u32[]{:S(2)}) collective-permute-start(bf16[64,768]{1,0:T(8,128)(2,1)S(1)} %get-tuple-element.55), channel_id=1, source_target_pairs={{0,3},{1,2},{2,1},{3,0},{4,7},{5,6},{6,5},{7,4},{8,11},{9,10},{10,... | collective-permute-start | bytes 294920 | tf_op jit(solution)/shard_map/ppermute | solution.py:409
  232.4 5.7 %collective-permute-start.42 = (bf16[64,768]{1,0:T(8,128)(2,1)S(1)}, bf16[64,768]{1,0:T(8,128)(2,1)S(1)}, u32[]{:S(2)}, u32[]{:S(2)}) collective-permute-start(bf16[64,768]{1,0:T(8,128)(2,1)S(1)} %get-tuple-element.56), channel_id=1, source_target_pairs={{0,4},{1,5},{2,6},{3,7},{4,0},{5,1},{6,2},{7,3},{8,12},{9,13},{10,... | collective-permute-start | bytes 294920 | tf_op jit(solution)/shard_map/ppermute | solution.py:409
  232.9 10.2 %collective-permute-start.43 = (bf16[64,768]{1,0:T(8,128)(2,1)S(1)}, bf16[64,768]{1,0:T(8,128)(2,1)S(1)}, u32[]{:S(2)}, u32[]{:S(2)}) collective-permute-start(bf16[64,768]{1,0:T(8,128)(2,1)S(1)} %get-tuple-element.57), channel_id=1, source_target_pairs={{0,5},{1,4},{2,7},{3,6},{4,1},{5,0},{6,3},{7,2},{8,13},{9,12},{10,... | collective-permute-start | bytes 294920 | tf_op jit(solution)/shard_map/ppermute | solution.py:409
  234.1 9.1 %collective-permute-start.44 = (bf16[64,768]{1,0:T(8,128)(2,1)S(1)}, bf16[64,768]{1,0:T(8,128)(2,1)S(1)}, u32[]{:S(2)}, u32[]{:S(2)}) collective-permute-start(bf16[64,768]{1,0:T(8,128)(2,1)S(1)} %get-tuple-element.58), channel_id=1, source_target_pairs={{0,6},{1,7},{2,4},{3,5},{4,2},{5,3},{6,0},{7,1},{8,14},{9,15},{10,... | collective-permute-start | bytes 294920 | tf_op jit(solution)/shard_map/ppermute | solution.py:409
  236.3 6.9 %collective-permute-start.45 = (bf16[64,768]{1,0:T(8,128)(2,1)S(1)}, bf16[64,768]{1,0:T(8,128)(2,1)S(1)}, u32[]{:S(2)}, u32[]{:S(2)}) collective-permute-start(bf16[64,768]{1,0:T(8,128)(2,1)S(1)} %get-tuple-element.59), channel_id=1, source_target_pairs={{0,7},{1,6},{2,5},{3,4},{4,3},{5,2},{6,1},{7,0},{8,15},{9,14},{10,... | collective-permute-start | bytes 294920 | tf_op jit(solution)/shard_map/ppermute | solution.py:409
where the time goes:
time: 245 us; the launch traced here: 244 us
  Pallas kernels  96.8 us (40%)
  waiting for transfers between devices  73.2 us (30%)
  starting transfers between devices  44.6 us (18%)
  local copies, waits for them, and re-layouts  28.1 us (11%)
    ppermute x46, waiting for transfers between devices, swap(): return lax.ppermute(value, axis, [(i, i ^ key) for i in range(count)])  73.2 us
    pallas_call x1, Pallas kernels, new_centroids(): pl.pallas_call(functools.partial(plan_kernel, planes=planes, owners=owner...  65 us
    ppermute x46, starting transfers between devices, swap(): return lax.ppermute(value, axis, [(i, i ^ key) for i in range(count)])  44.6 us
    unnamed x23, local copies, waits for them, and re-layouts  24.8 us
    pallas_call x1, Pallas kernels, logits_and_stats(): pl.pallas_call(functools.partial(logits_kernel, chunk=min(256, rows)), gr...  11.1 us
    pallas_call x1, Pallas kernels, first_rows(): pl.pallas_call(functools.partial(first_rows_kernel, parts=len(stats), log...  8.63 us
    pallas_call x2, Pallas kernels, row_sums(): pl.pallas_call(functools.partial(row_sum_kernel, parts=len(stats), ratio=...  6.32 us
  transfers between devices with their start and end apart: 46, of which 23 were waited for; matrix products, arithmetic and copies ran while one was open for 4% of the time, Pallas kernels for 4%

commit v1 on v0

--- a/solution.py
+++ b/solution.py
@@ -17,6 +17,7 @@
 NT = (((1,), (1,)), ((), ()))
 NN = (((1,), (0,)), ((), ()))
 MIB = 1 << 20
+OWN_TILE = 1024
 
 
 def cost(flops, moved, exps=0):
@@ -94,7 +95,7 @@
 def first_rows_kernel(*refs, parts, log_mass, group):
     l_ref, ids_ref = refs[0:2]
     stats = refs[2 : 2 + parts]
-    m_ref, stat_ref, col_ref, peaks, totals = refs[2 + parts :]
+    m_ref, stat_ref, col_ref, spare_ref, peaks, totals = refs[2 + parts :]
 
     @pl.when(pl.program_id(0) == 0)
     def _():
@@ -108,7 +109,9 @@
         shifted = l_ref[rows, :] + col_ref[...]
         peak = jnp.max(shifted, axis=1, keepdims=True)
         scaled = jnp.exp(shifted - peak)
-        m_ref[rows, :] = scaled.astype(BF16)
+        rounded = scaled.astype(BF16)
+        m_ref[rows, :] = rounded
+        spare_ref[rows, :] = rounded
         peaks[rows, :] = jnp.broadcast_to(peak, (group, 128))
         totals[rows, :] = jnp.broadcast_to(jnp.sum(scaled, axis=1, keepdims=True), (group, 128))
         return carry
@@ -121,9 +124,9 @@
 
 def first_rows(logits, ids, stats, log_mass):
     rows, lists = logits.shape
-    tile = min(256, rows)
-    return pl.pallas_call(
-        functools.partial(first_rows_kernel, parts=len(stats), log_mass=log_mass, group=16),
+    tile = min(512, rows)
+    return pl.pallas_call(
+        functools.partial(first_rows_kernel, parts=len(stats), log_mass=log_mass, group=32),
         grid=(rows // tile,),
         in_specs=[
             pl.BlockSpec((tile, lists), lambda i: (i, 0)),
@@ -134,14 +137,16 @@
             pl.BlockSpec((tile, lists), lambda i: (i, 0)),
             pl.BlockSpec((3, tile), lambda i: (0, i)),
             whole((1, lists)),
+            pl.BlockSpec((tile, lists), lambda i: (i, 0)),
         ],
         out_shape=[
             pltpu.VMEM((rows, lists), BF16),
             jax.ShapeDtypeStruct((3, rows), F32),
             jax.ShapeDtypeStruct((1, lists), F32),
+            pltpu.HBM((rows, lists), BF16),
         ],
         scratch_shapes=[pltpu.VMEM((tile, 128), F32), pltpu.VMEM((tile, 128), F32)],
-        compiler_params=grant(16),
+        compiler_params=grant(24),
         cost_estimate=cost(4 * rows * lists, 6 * rows * lists, rows * lists),
         name="first_rows",
     )(in_vmem(logits), ids, *stats)
@@ -163,11 +168,11 @@
 def column_sum_kernel(*refs, parts, first):
     m_ref, own_ref = refs[0:2]
     stats = refs[2 : 2 + parts]
+    weights = refs[-1]
     if first:
-        out_ref, peak_ref, _, weights = refs[2 + parts :]
+        out_ref, peak_ref = refs[2 + parts : 4 + parts]
     else:
-        peak_ref = refs[2 + parts]
-        out_ref, _, weights = refs[3 + parts :]
+        peak_ref, out_ref = refs[2 + parts : 4 + parts]
 
     @pl.when(pl.program_id(0) == 0)
     def _():
@@ -184,7 +189,7 @@
     )
 
 
-def column_sums(scaled, own, stats, peak=None):
+def column_sums(scaled, own, stats, last, peak=None):
     rows, lists = scaled.shape
     tile = min(512, lists)
     first = peak is None
@@ -198,11 +203,11 @@
         in_specs=[pl.BlockSpec((rows, tile), lambda j: (0, j)), whole(own.shape)]
         + [whole(stats[0].shape)] * len(stats)
         + ([] if first else [row]),
-        out_specs=out_specs + ([row] if first else []) + [kept],
+        out_specs=out_specs + ([row] if first else []) + ([] if last else [kept]),
         out_shape=out_shape
         + ([jax.ShapeDtypeStruct((1, rows), F32)] if first else [])
-        + [pltpu.VMEM(scaled.shape, scaled.dtype)],
-        input_output_aliases={0: 2 if first else 1},
+        + ([] if last else [pltpu.VMEM(scaled.shape, scaled.dtype)]),
+        input_output_aliases={} if last else {0: 2 if first else 1},
         scratch_shapes=[pltpu.VMEM((8, rows), BF16)],
         compiler_params=grant(16),
         cost_estimate=cost(16 * rows * lists, 2 * rows * lists),
@@ -213,7 +218,7 @@
 def row_sum_kernel(*refs, parts, ratio, log_mass):
     m_ref, first_ref, own_ref, peak_ref = refs[0:4]
     stats = refs[4 : 4 + parts]
-    out_ref, col_ref, _, weights = refs[4 + parts :]
+    out_ref, col_ref, weights = refs[4 + parts], refs[5 + parts], refs[-1]
 
     @pl.when(pl.program_id(0) == 0)
     def _():
@@ -225,7 +230,7 @@
     out_ref[...] = sums * jnp.exp(own_ref[0:1, :] - peak_ref[...])
 
 
-def row_sums(scaled, first_column, own, peak, stats, ratio):
+def row_sums(scaled, first_column, own, peak, stats, ratio, last):
     rows, lists = scaled.shape
     tile = min(512, rows)
     column = whole((1, lists))
@@ -244,139 +249,218 @@
         out_specs=[
             pl.BlockSpec((1, tile), lambda i: (0, i)),
             column,
-            pl.BlockSpec(memory_space=pl.ANY),
-        ],
+        ]
+        + ([] if last else [pl.BlockSpec(memory_space=pl.ANY)]),
         out_shape=[
             jax.ShapeDtypeStruct((1, rows), F32),
             jax.ShapeDtypeStruct((1, lists), F32),
-            pltpu.VMEM(scaled.shape, scaled.dtype),
-        ],
-        input_output_aliases={0: 2},
+        ]
+        + ([] if last else [pltpu.VMEM(scaled.shape, scaled.dtype)]),
+        input_output_aliases={} if last else {0: 2},
         scratch_shapes=[pltpu.VMEM((8, lists), BF16)],
         compiler_params=grant(16),
         cost_estimate=cost(16 * rows * lists, 2 * rows * lists),
         name="row_sums",
-    )(in_vmem(scaled), first_column, own, peak, *stats)
-
-
-def plan_kernel(*refs, planes, owners, depth):
-    place_ref, c_ref, col_ref = refs[0:3]
-    rows_in = refs[3 : 3 + planes]
-    own_ref = refs[3 + planes]
-    halves = refs[4 + planes : 4 + planes + 2 * (planes - 1)]
-    ids_ref, out_ref = refs[4 + planes + 2 * (planes - 1) : 6 + planes + 2 * (planes - 1)]
-    picked = refs[6 + planes + 2 * (planes - 1) : -6]
-    held, row_all, acc, mass, chosen, sems = refs[-6:]
-    tile = c_ref.shape[0]
-    count = own_ref.shape[0]
-    piece = count // owners
-    plane, owner = place_ref[0], place_ref[1]
-
-    def block(index):
-        return pl.ds(pl.multiple_of(index * count, count), count)
-
-    @pl.when(pl.program_id(0) == 0)
-    def _():
-        pltpu.make_async_copy(own_ref, held.at[block(plane)], sems.at[0]).start()
-        row_all[pl.ds(plane, 1), :] = rows_in[0][...]
-        for key in range(1, planes):
-            other = plane ^ key
-            row_all[pl.ds(other, 1), :] = rows_in[key][...]
-            for index in range(owners):
-                source = halves[2 * (key - 1) + index // (owners // 2)]
-                at = (index % (owners // 2)) * piece
-                slot = 2 * (index % (owners // 2)) + index // (owners // 2)
-                start = pl.multiple_of(other * count + (owner ^ slot) * piece, piece)
-                pltpu.make_async_copy(
-                    source.at[pl.ds(at, piece)], held.at[pl.ds(start, piece)], sems.at[key]
-                ).start()
-
-    doubled = c_ref[...] * 2
-    column = jnp.transpose(jnp.broadcast_to(col_ref[...], (128, tile)))[:, 0:1]
-    steps = planes * count // depth
-
-    def logits(step):
-        here = held[step * depth : (step + 1) * depth, :]
-        return lax.dot_general(doubled, here, NT, preferred_element_type=F32)
-
-    @pl.when(pl.program_id(0) == 0)
-    def _():
-        for key in range(planes):
-            pltpu.make_async_copy(held.at[block(key)], held.at[block(key)], sems.at[key]).wait()
-
-    ready = logits(0)
-    for step in range(steps):
-        following = logits(step + 1) if step + 1 < steps else None
-        start = step * depth
-        row = row_all[start // count : start // count + 1, start % count : start % count + depth]
-        plan = jnp.exp(ready + row + column).astype(BF16)
-        part = lax.dot_general(
-            plan, held[start : start + depth, :], NN, preferred_element_type=F32
-        )
+    )(in_hbm(scaled) if last else in_vmem(scaled), first_column, own, peak, *stats)
+
+
+def block_sums(blocks):
+    flat = [(index, item) for index, block in enumerate(blocks) for item in block]
+
+    def logits(item):
+        return lax.dot_general(item[0], item[2](), NT, preferred_element_type=F32)
+
+    found = [None] * len(blocks)
+    ready = logits(flat[0][1])
+    for place, (index, item) in enumerate(flat):
+        following = logits(flat[place + 1][1]) if place + 1 < len(flat) else None
+        plan = jnp.exp(ready + item[3]() + item[1]).astype(BF16)
+        part = lax.dot_general(plan, item[2](), NN, preferred_element_type=F32)
         wide = plan.astype(F32)
         sums = wide[:, 0:128]
-        for lane in range(128, depth, 128):
+        for lane in range(128, wide.shape[1], 128):
             sums = sums + wide[:, lane : lane + 128]
-        acc[...] = part if step == 0 else acc[...] + part
-        mass[...] = sums if step == 0 else mass[...] + sums
+        before = found[index]
+        found[index] = (part, sums) if before is None else (before[0] + part, before[1] + sums)
         ready = following
-    fresh = (acc[...] / jnp.sum(mass[...], axis=1, keepdims=True)).astype(BF16)
-    out_ref[...] = fresh
+    return found
+
+
+def chunk(index, depth):
+    return slice(index * depth, (index + 1) * depth)
+
+
+def wide_column(col_ref):
+    size = col_ref.shape[1]
+    return jnp.transpose(jnp.broadcast_to(col_ref[...], (128, size)))[:, 0:1]
+
+
+def loads(ref, rows, columns):
+    return lambda: ref[rows, columns]
+
+
+def own_plan_kernel(c_ref, col_ref, v_ref, r_ref, sum_ref, mass_ref, *, depth, part):
+    doubled, column = c_ref[...] * 2, wide_column(col_ref)
+    every = slice(None)
+    parts = [slice(start, start + part) for start in range(0, doubled.shape[0], part)]
+    blocks = [
+        [
+            (
+                doubled[here],
+                column[here],
+                loads(v_ref, chunk(step, depth), every),
+                loads(r_ref, every, chunk(step, depth)),
+            )
+            for step in range(v_ref.shape[0] // depth)
+        ]
+        for here in parts
+    ]
+    for here, (total, weight) in zip(parts, block_sums(blocks)):
+        sum_ref[here, :] = total
+        mass_ref[here, :] = weight
+
+
+def own_plan(centroids, column, vectors, row):
+    count, width = vectors.shape
+    lists = centroids.shape[0]
+    tile, depth = min(OWN_TILE, lists), min(1024, count)
+    return pl.pallas_call(
+        functools.partial(own_plan_kernel, depth=depth, part=min(256, lists)),
+        grid=(lists // tile,),
+        in_specs=[
+            pl.BlockSpec((tile, width), lambda j: (j, 0)),
+            pl.BlockSpec((1, tile), lambda j: (0, j)),
+            whole((count, width)),
+            whole((1, count)),
+        ],
+        out_specs=[
+            pl.BlockSpec((tile, width), lambda j: (j, 0)),
+            pl.BlockSpec((tile, 128), lambda j: (j, 0)),
+        ],
+        out_shape=[
+            pltpu.HBM((lists, width), F32),
+            pltpu.HBM((lists, 128), F32),
+        ],
+        compiler_params=grant(40),
+        cost_estimate=cost(4 * count * lists * width, 4 * lists * width, count * lists),
+        name="own_plan",
+    )(in_hbm(centroids), column, in_hbm(vectors), row)
+
+
+def plan_kernel(*refs, planes, owners, depth):
+    others = planes - 1
+    place_ref, c_ref, col_ref, sum_ref, mass_ref, ids_ref = refs[0:6]
+    rows_in = refs[6 : 6 + others]
+    halves = refs[6 + others : 6 + 3 * others]
+    out_ref = refs[6 + 3 * others]
+    picked = refs[7 + 3 * others : -3]
+    held, chosen, sems = refs[-3:]
+    tile = c_ref.shape[0]
+    count = held.shape[0] // others
+    piece = count // owners
     turn = pl.program_id(0)
-    slots = ids_ref.shape[0]
-    lanes = lax.broadcasted_iota(jnp.int32, (slots, tile), 1) + turn * tile
-    wanted = (ids_ref[...] == lanes).astype(F32).astype(BF16)
-    some = lax.dot_general(wanted, fresh, NN, preferred_element_type=F32)
+
+    def copies(key):
+        for index in range(owners):
+            source = halves[2 * (key - 1) + index // (owners // 2)]
+            at = (index % (owners // 2)) * piece
+            slot = 2 * (index % (owners // 2)) + index // (owners // 2)
+            start = (key - 1) * count + (place_ref[0] ^ slot) * piece
+            yield pltpu.make_async_copy(
+                source.at[pl.ds(at, piece)],
+                held.at[pl.ds(pl.multiple_of(start, piece), piece)],
+                sems.at[key - 1],
+            )
+
+    def wait(key):
+        here = held.at[pl.ds((key - 1) * count, count)]
+        pltpu.make_async_copy(here, here, sems.at[key - 1]).wait()
+
+    def compute():
+        doubled, column = c_ref[...] * 2, wide_column(col_ref)
+        steps = count // depth
+        every = slice(None)
+        blocks = [
+            [
+                (
+                    doubled,
+                    column,
+                    loads(held, chunk((key - 1) * steps + step, depth), every),
+                    loads(rows_in[key - 1], every, chunk(step, depth)),
+                )
+                for step in range(steps)
+            ]
+            for key in range(1, planes)
+        ]
+        found = [(sum_ref[...], mass_ref[...])] + block_sums(blocks)
+        numerator = tree([item[0] for item in found], jnp.add)
+        weight = tree([item[1] for item in found], jnp.add)
+        fresh = (numerator / jnp.sum(weight, axis=1, keepdims=True)).astype(BF16)
+        out_ref[...] = fresh
+        slots = ids_ref.shape[0]
+        lanes = lax.broadcasted_iota(jnp.int32, (slots, tile), 1) + turn * tile
+        wanted = (ids_ref[...] == lanes).astype(F32).astype(BF16)
+        return lax.dot_general(wanted, fresh, NN, preferred_element_type=F32)
 
     @pl.when(turn == 0)
     def _():
-        chosen[...] = some
-
-    @pl.when(turn > 0)
-    def _():
-        chosen[...] += some
+        for key in range(1, planes):
+            for copy in copies(key):
+                copy.start()
+        chosen[...] = jnp.zeros_like(chosen)
+        for key in range(1, planes):
+            wait(key)
+
+    chosen[...] += compute()
 
     @pl.when(turn == pl.num_programs(0) - 1)
     def _():
-        each = slots // len(picked)
+        each = ids_ref.shape[0] // len(picked)
         for index, piece_ref in enumerate(picked):
             piece_ref[...] = chosen[index * each : (index + 1) * each, :].astype(BF16)
 
 
-def new_centroids(place, centroids, column, rows, own, halves, ids, owners):
-    count, width = own.shape
-    lists = centroids.shape[0]
-    planes = len(rows)
+def new_centroids(place, centroids, column, sums, masses, ids, rows, halves, owners):
+    lists, width = centroids.shape
+    others = len(rows)
+    count = rows[0].shape[1]
     tile, depth = min(256, lists), min(1024, count)
-    anywhere = pl.BlockSpec(memory_space=pl.ANY)
-    total = planes * count
-    return pl.pallas_call(
-        functools.partial(plan_kernel, planes=planes, owners=owners, depth=depth),
+    total = others * count
+    return pl.pallas_call(
+        functools.partial(plan_kernel, planes=others + 1, owners=owners, depth=depth),
         grid=(lists // tile,),
         in_specs=[
             pl.BlockSpec(memory_space=pltpu.SMEM),
             pl.BlockSpec((tile, width), lambda j: (j, 0)),
             pl.BlockSpec((1, tile), lambda j: (0, j)),
+            pl.BlockSpec((tile, width), lambda j: (j, 0)),
+            pl.BlockSpec((tile, 128), lambda j: (j, 0)),
+            whole(ids.shape),
         ]
-        + [whole((1, count))] * planes
-        + [anywhere] * (1 + len(halves))
-        + [whole(ids.shape)],
+        + [whole((1, count))] * others
+        + [pl.BlockSpec(memory_space=pl.ANY)] * len(halves),
         out_specs=[pl.BlockSpec((tile, width), lambda j: (j, 0))]
         + [whole((ids.shape[0] // owners, width))] * owners,
         out_shape=[jax.ShapeDtypeStruct((lists, width), BF16)]
         + [jax.ShapeDtypeStruct((ids.shape[0] // owners, width), BF16)] * owners,
         scratch_shapes=[
             pltpu.VMEM((total, width), BF16),
-            pltpu.VMEM((max(8, planes), count), F32),
-            pltpu.VMEM((tile, width), F32),
-            pltpu.VMEM((tile, 128), F32),
             pltpu.VMEM((ids.shape[0], width), F32),
-            pltpu.SemaphoreType.DMA((planes,)),
+            pltpu.SemaphoreType.DMA((others,)),
         ],
         compiler_params=grant(40),
         cost_estimate=cost(4 * total * lists * width, 2 * total * width, total * lists),
         name="new_centroids",
-    )(place, in_hbm(centroids), column, *rows, in_hbm(own), *halves, ids)
+    )(
+        place,
+        in_hbm(centroids),
+        column,
+        in_hbm(sums),
+        in_hbm(masses),
+        ids,
+        *rows,
+        *[in_hbm(half) for half in halves],
+    )
 
 
 def residual_kernel(*refs):
@@ -404,6 +488,34 @@
     )(slots, own, *pieces)
 
 
+def join_kernel(*refs):
+    pieces, out_ref, sems = refs[:-2], refs[-2], refs[-1]
+    each = pieces[0].shape[0]
+    moves = [
+        pltpu.make_async_copy(piece, out_ref.at[pl.ds(index * each, each)], sems.at[index])
+        for index, piece in enumerate(pieces)
+    ]
+    for move in moves:
+        move.start()
+    for move in moves:
+        move.wait()
+
+
+def join_pieces(pieces):
+    each, width = pieces[0].shape
+    anywhere = pl.BlockSpec(memory_space=pl.ANY)
+    return pl.pallas_call(
+        join_kernel,
+        in_specs=[anywhere] * len(pieces),
+        out_specs=anywhere,
+        out_shape=pltpu.HBM((each * len(pieces), width), pieces[0].dtype),
+        scratch_shapes=[pltpu.SemaphoreType.DMA((len(pieces),))],
+        compiler_params=grant(4),
+        cost_estimate=cost(0, 2 * each * len(pieces) * width),
+        name="join_pieces",
+    )(*[in_vmem(piece) for piece in pieces])
+
+
 def swap(value, axis, key):
     count = lax.axis_size(axis)
     return lax.ppermute(value, axis, [(i, i ^ key) for i in range(count)])
@@ -423,7 +535,7 @@
     data_count = lax.axis_size("dp")
     owner_count = lax.axis_size("cent")
     me = lax.axis_index("cent")
-    place = jnp.stack([lax.axis_index("dp"), me]).astype(jnp.int32)
+    place = me.astype(jnp.int32)[None]
     send_count = row_count // owner_count
     capacity = max(2, 2 * send_count // owner_count)
     slot_count = owner_count * capacity
@@ -444,16 +556,16 @@
         return everywhere(after(piece, *ready), "cent", 2)
 
     def partners(pieces):
-        half = jnp.concatenate(pieces, axis=0)
+        half = join_pieces(pieces)
         return [half, swap(half, "cent", 1)]
 
     arriving = [swap(own, "dp", 1)]
     logits, stats = logits_and_stats(vectors, centroids)
     parts = everywhere(stats, "dp")
     if data_count > 2:
-        arriving.append(swap(after(own, stats), "dp", 2))
+        arriving.append(swap(after(own, *parts), "dp", 2))
     moved = across(arriving[0], stats)
-    scaled, own_stats, first_column = first_rows(logits, ids_row, parts, log_mass)
+    scaled, own_stats, first_column, spare = first_rows(logits, ids_row, parts, log_mass)
     partner = swap(own_stats, "cent", 1)
     pair = jnp.concatenate(
         join_pairs([own_stats, partner]) + (own_stats[2:3], partner[2:3]), axis=0
@@ -469,15 +581,18 @@
     for turn in range(1, ITERS):
         halves += partners(moved)
         moved = across(arriving[turn], pair)
-        if turn == 1:
-            sums, peak, scaled = column_sums(scaled, own_stats, parts)
-        else:
-            sums, scaled = column_sums(scaled, own_stats, parts, peak)
+        last = turn == ITERS - 1
+        sums, *kept = column_sums(scaled, own_stats, parts, last, peak)
+        peak = kept.pop(0) if turn == 1 else peak
+        scaled = scaled if last else kept[0]
         parts = everywhere(sums, "dp")
         if turn == 1:
             for key in range(3, data_count):
-                arriving.append(swap(after(own, sums), "dp", key))
-        sums, column, scaled = row_sums(scaled, first_column, own_stats, peak, parts, ratio)
+                arriving.append(swap(after(own, *parts), "dp", key))
+        sums, column, *kept = row_sums(
+            spare if last else scaled, first_column, own_stats, peak, parts, ratio, last
+        )
+        scaled = scaled if last else kept[0]
         partner = swap(sums, "cent", 1)
         pair = sums + partner
         parts = everywhere(pair, "cent", 2)
@@ -486,9 +601,18 @@
         halves += partners(across(arriving[turn]))
     row = -(peak + jnp.log(tree(parts, jnp.add)))
 
-    rows = everywhere(row, "dp")
+    rows = everywhere(row, "dp")[1:]
+    sums, masses = own_plan(centroids, column, vectors, row)
     updated, *pieces = new_centroids(
-        place, centroids, column, rows, vectors, halves, arrived[:, None], owner_count
+        place,
+        centroids,
+        column,
+        sums,
+        masses,
+        arrived[:, None],
+        rows,
+        halves,
+        owner_count,
     )
     pieces = [pieces[0]] + [swap(pieces[key], "cent", key) for key in range(1, owner_count)]
     residuals = subtract_rows(slots[:, None], own, pieces)

time: 245 us -> 250 us (1.020)
  local copies, waits for them, and re-layouts: 28.1 us -> 14 us
  starting transfers between devices: 44.6 us -> 55.4 us
  Pallas kernels: 96.8 us -> 106 us
    unnamed x23 -> x12, local copies, waits for them, and re-layouts: 24.8 us -> 12.3 us
    ppermute x46, starting transfers between devices: 44.6 us -> 55.4 us  [swap(): return lax.ppermute(value, axis, [(i, i ^ key) for i in range(count)])]
    pallas_call x1 -> x5, Pallas kernels: 65 us -> 72.7 us  [the longest x1 50.7 us: new_centroids(): pl.pallas_call(functools.partial(plan_kernel, planes=others + 1, owners=o...]
    pallas_call x2, Pallas kernels: 6.32 us -> 8.98 us  [row_sums(): pl.pallas_call(functools.partial(row_sum_kernel, parts=len(stats), ratio=...]
  transfers between devices with their start and end apart: 46 -> 46, of which waited for: 23 -> 21; matrix products, arithmetic and copies ran while one was open for 4% -> 1% of each run, Pallas kernels for 4% -> 14%
where the time goes in v1:
time: 250 us
  Pallas kernels  106 us (42%)
  waiting for transfers between devices  73.4 us (29%)
  starting transfers between devices  55.4 us (22%)
  local copies, waits for them, and re-layouts  14 us (6%)
    ppermute x46, waiting for transfers between devices, swap(): return lax.ppermute(value, axis, [(i, i ^ key) for i in range(count)])  73.4 us
    ppermute x46, starting transfers between devices, swap(): return lax.ppermute(value, axis, [(i, i ^ key) for i in range(count)])  55.4 us
    pallas_call x1, Pallas kernels, new_centroids(): pl.pallas_call(functools.partial(plan_kernel, planes=others + 1, owners=o...  50.7 us
    pallas_call x1, Pallas kernels, own_plan(): pl.pallas_call(functools.partial(own_plan_kernel, depth=depth, part=min(2...  18.3 us
    unnamed x12, local copies, waits for them, and re-layouts  12.3 us
    pallas_call x1, Pallas kernels, logits_and_stats(): pl.pallas_call(functools.partial(logits_kernel, chunk=min(256, rows)), gr...  11.1 us
    pallas_call x2, Pallas kernels, row_sums(): pl.pallas_call(functools.partial(row_sum_kernel, parts=len(stats), ratio=...  8.98 us
    pallas_call x1, Pallas kernels, first_rows(): pl.pallas_call(functools.partial(first_rows_kernel, parts=len(stats), log...  7.02 us
  transfers between devices with their start and end apart: 46, of which 21 were waited for; matrix products, arithmetic and copies ran while one was open for 1% of the time, Pallas kernels for 14%

profile of v1, /device:TPU:0, one launch (start us, length us, event | category | flops | bytes accessed | tf_op | source)
XLA Modules:
  0.0 249.9 jit_solution(5261466074439135176)
XLA Ops:
  0.6 11.1 %logits_stats.1 = (f32[2048,2048]{1,0:T(8,128)S(1)}, f32[2,2048]{1,0:T(2,128)S(1)}) custom-call(bf16[2048,768]{1,0:T(8,128)(2,1)} %v_ref.3, bf16[2048,768]{1,0:T(8,128)(2,1)} %refs_1_.1), custom_call_target="tpu_custom_call" | custom-call | flops 6442450944 | bytes 16777216 | tf_op jit(solution)/shard_map/logits_stats/pallas_call | solution.py:77
  11.7 5.8 %copy-done = f32[2048,2048]{1,0:T(8,128)} copy-done((f32[2048,2048]{1,0:T(8,128)}, f32[2048,2048]{1,0:T(8,128)S(1)}, u32[]{:S(2)}) %copy-start) | copy-done | bytes 16777240
  17.5 3.1 %collective-permute-start = (f32[2,2048]{1,0:T(2,128)S(1)}, f32[2,2048]{1,0:T(2,128)S(1)}, u32[]{:S(2)}, u32[]{:S(2)}) collective-permute-start(f32[2,2048]{1,0:T(2,128)S(1)} %get-tuple-element.34.refs_2_), channel_id=1, source_target_pairs={{0,8},{8,0},{16,24},{24,16},{1,9},{9,1},{17,25},{25,17},{2,10},{10... | collective-permute-start | bytes 49160 | tf_op jit(solution)/shard_map/ppermute | solution.py:521
  20.5 2.6 %collective-permute-start.1 = (f32[2,2048]{1,0:T(2,128)S(1)}, f32[2,2048]{1,0:T(2,128)S(1)}, u32[]{:S(2)}, u32[]{:S(2)}) collective-permute-start(f32[2,2048]{1,0:T(2,128)S(1)} %get-tuple-element.34.refs_2_), channel_id=1, source_target_pairs={{0,16},{8,24},{16,0},{24,8},{1,17},{9,25},{17,1},{25,9},{2,18},{10... | collective-permute-start | bytes 49160 | tf_op jit(solution)/shard_map/ppermute | solution.py:521
  23.7 1.6 collective-permute-done.1.refs_4_
  25.3 3.4 %collective-permute-done.2.refs_5_ = f32[2,2048]{1,0:T(2,128)S(1)} collective-permute-done((f32[2,2048]{1,0:T(2,128)S(1)}, f32[2,2048]{1,0:T(2,128)S(1)}, u32[]{:S(2)}, u32[]{:S(2)}) %collective-permute-start.2) | collective-permute-done | bytes 16416 | tf_op jit(solution)/shard_map/ppermute | solution.py:521
  28.7 5.8 %copy-done.1 = f32[2048,2048]{1,0:T(8,128)S(1)} copy-done((f32[2048,2048]{1,0:T(8,128)S(1)}, f32[2048,2048]{1,0:T(8,128)}, u32[]{:S(2)}) %copy-start.1) | copy-done | bytes 16777240
  34.4 7.0 %first_rows.1 = (bf16[2048,2048]{1,0:T(8,128)(2,1)S(1)}, f32[3,2048]{1,0:T(4,128)S(1)}, f32[1,2048]{1,0:T(1,128)S(1)}, bf16[2048,2048]{1,0:T(8,128)(2,1)}) custom-call(f32[2048,2048]{1,0:T(8,128)S(1)} %copy-done.1, f32[1,2048]{1,0:T(1,128)S(1)} %bitcast.21, f32[2,2048]{1,0:T(2,128)S(1)} %get-tuple-element.34.refs_2_, ...), custom_call_target="tpu_custom_call" | custom-call | flops 16777216 | bytes 25165824 | tf_op jit(solution)/shard_map/first_rows/pallas_call | solution.py:128
  41.5 1.0 constant_dynamic-slice_fusion.refs_1_
  42.8 1.6 collective-permute-start.4
  44.3 1.5 collective-permute-start.5
  46.7 1.5 collective-permute-done.5.refs_4_
  48.2 2.4 collective-permute-done.6.refs_5_
  50.6 2.3 column_sums.2
  53.0 1.9 collective-permute-start.7
  54.9 2.5 collective-permute-start.9
  57.8 14.2 %collective-permute-done.8.refs_6_ = f32[1,2048]{1,0:T(1,128)S(1)} collective-permute-done((f32[1,2048]{1,0:T(1,128)S(1)}, f32[1,2048]{1,0:T(1,128)S(1)}, u32[]{:S(2)}, u32[]{:S(2)}) %collective-permute-start.8) | collective-permute-done | bytes 8224 | tf_op jit(solution)/shard_map/ppermute | solution.py:521
  72.0 0.6 collective-permute-start.25
  73.1 3.2 %row_sums.2 = (f32[1,2048]{1,0:T(1,128)S(1)}, f32[1,2048]{1,0:T(1,128)}, bf16[2048,2048]{1,0:T(8,128)(2,1)S(1)}) custom-call(bf16[2048,2048]{1,0:T(8,128)(2,1)S(1)} %get-tuple-element.40.refs_0_, f32[1,2048]{1,0:T(1,128)S(1)} %get-tuple-element.36.refs_1_, f32[3,2048]{1,0:T(4,128)S(1)} %get-tuple-element.37.refs_1_.refs_2_, ...), custom_call_target="tpu_custom_call", output_to_operand_aliasing={{2}: (0, {})} | custom-call | flops 67108864 | bytes 8388608 | tf_op jit(solution)/shard_map/row_sums/pallas_call | solution.py:237
  76.3 1.2 collective-permute-done.10
  77.5 1.6 collective-permute-start.11
  79.0 2.2 collective-permute-done.11.refs_3_
  81.2 1.5 collective-permute-start.12
  82.7 2.1 collective-permute-done.12.refs_4_
  84.8 2.4 collective-permute-start.13
  87.3 2.1 collective-permute-done.13.refs_5_
  89.4 2.3 column_sums.3.refs_4_
  91.7 1.0 collective-permute-start.14
  92.7 2.6 %collective-permute-done.14.refs_5_ = f32[1,2048]{1,0:T(1,128)S(1)} collective-permute-done((f32[1,2048]{1,0:T(1,128)S(1)}, f32[1,2048]{1,0:T(1,128)S(1)}, u32[]{:S(2)}, u32[]{:S(2)}) %collective-permute-start.14) | collective-permute-done | bytes 8224 | tf_op jit(solution)/shard_map/ppermute | solution.py:521
  95.3 2.3 collective-permute-start.15
  97.6 2.3 collective-permute-done.15.refs_6_
  99.9 3.8 %collective-permute-start.16 = (f32[1,2048]{1,0:T(1,128)S(1)}, f32[1,2048]{1,0:T(1,128)S(1)}, u32[]{:S(2)}, u32[]{:S(2)}) collective-permute-start(f32[1,2048]{1,0:T(1,128)S(1)} %column_sums.3.refs_4_), channel_id=1, source_target_pairs={{0,24},{8,16},{16,8},{24,0},{1,25},{9,17},{17,9},{25,1},{2,26},{10... | collective-permute-start | bytes 24584 | tf_op jit(solution)/shard_map/ppermute | solution.py:521
  103.6 1.7 collective-permute-done.16.refs_7_
  105.3 5.8 %row_sums.3 = (f32[1,2048]{1,0:T(1,128)S(1)}, f32[1,2048]{1,0:T(1,128)}) custom-call(bf16[2048,2048]{1,0:T(8,128)(2,1)} %get-tuple-element.35.refs_0_, f32[1,2048]{1,0:T(1,128)S(1)} %get-tuple-element.36.refs_1_, f32[3,2048]{1,0:T(4,128)S(1)} %get-tuple-element.37.refs_1_.refs_2_, f32[1,2048]{1,0:T(1,128)S(1)} %get-tuple-element.39.refs_3_.refs_6_, ...), custom_call_target="tpu_custom_call" | custom-call | flops 67108864 | bytes 8388608 | tf_op jit(solution)/shard_map/row_sums/pallas_call | solution.py:237
  111.2 2.5 collective-permute-start.27
  113.6 0.5 collective-permute-start.30
  114.2 0.5 collective-permute-start.31
  114.7 2.4 collective-permute-start.32
  117.1 0.5 collective-permute-start.35
  117.7 6.4 %collective-permute-done.27.refs_3_ = bf16[256,768]{1,0:T(8,128)(2,1)S(1)} collective-permute-done((bf16[256,768]{1,0:T(8,128)(2,1)S(1)}, bf16[256,768]{1,0:T(8,128)(2,1)S(1)}, u32[]{:S(2)}, u32[]{:S(2)}) %collective-permute-start.27) | collective-permute-done | bytes 393248 | tf_op jit(solution)/shard_map/ppermute | solution.py:521
  124.1 1.5 collective-permute-start.36
  125.6 7.0 %collective-permute-done.30.refs_1_ = bf16[256,768]{1,0:T(8,128)(2,1)S(1)} collective-permute-done((bf16[256,768]{1,0:T(8,128)(2,1)S(1)}, bf16[256,768]{1,0:T(8,128)(2,1)S(1)}, u32[]{:S(2)}, u32[]{:S(2)}) %collective-permute-start.30) | collective-permute-done | bytes 393248 | tf_op jit(solution)/shard_map/ppermute | solution.py:521
  132.6 1.4 collective-permute-start.37
  134.1 0.6 collective-permute-start.18
  134.7 6.3 %collective-permute-done.32.refs_3_ = bf16[256,768]{1,0:T(8,128)(2,1)S(1)} collective-permute-done((bf16[256,768]{1,0:T(8,128)(2,1)S(1)}, bf16[256,768]{1,0:T(8,128)(2,1)S(1)}, u32[]{:S(2)}, u32[]{:S(2)}) %collective-permute-start.32) | collective-permute-done | bytes 393248 | tf_op jit(solution)/shard_map/ppermute | solution.py:521
  141.0 1.5 collective-permute-start.19
  142.5 7.0 %collective-permute-done.35.refs_1_ = bf16[256,768]{1,0:T(8,128)(2,1)S(1)} collective-permute-done((bf16[256,768]{1,0:T(8,128)(2,1)S(1)}, bf16[256,768]{1,0:T(8,128)(2,1)S(1)}, u32[]{:S(2)}, u32[]{:S(2)}) %collective-permute-start.35) | collective-permute-done | bytes 393248 | tf_op jit(solution)/shard_map/ppermute | solution.py:521
  149.5 1.4 collective-permute-start.20
  151.0 1.3 join_pieces.3.refs_9_
  152.3 1.2 join_pieces.4.refs_11_
  153.5 0.7 copy-done.4
  154.3 3.3 %collective-permute-done.37.refs_3_ = bf16[256,768]{1,0:T(8,128)(2,1)S(1)} collective-permute-done((bf16[256,768]{1,0:T(8,128)(2,1)S(1)}, bf16[256,768]{1,0:T(8,128)(2,1)S(1)}, u32[]{:S(2)}, u32[]{:S(2)}) %collective-permute-start.37) | collective-permute-done | bytes 393248 | tf_op jit(solution)/shard_map/ppermute | solution.py:521
  157.6 1.2 join_pieces.5.refs_13_
  158.8 0.6 collective-permute-start.38
  159.8 4.4 %collective-permute-start.22 = (f32[1,2048]{1,0:T(1,128)S(1)}, f32[1,2048]{1,0:T(1,128)S(1)}, u32[]{:S(2)}, u32[]{:S(2)}) collective-permute-start(f32[1,2048]{1,0:T(1,128)S(1)} %add_negate_fusion.r_ref), channel_id=1, source_target_pairs={{0,16},{8,24},{16,0},{24,8},{1,17},{9,25},{17,1},{25,9},{2,18},{10... | collective-permute-start | bytes 24584 | tf_op jit(solution)/shard_map/ppermute | solution.py:521
  164.2 2.7 %collective-permute-start.23 = (f32[1,2048]{1,0:T(1,128)S(1)}, f32[1,2048]{1,0:T(1,128)S(1)}, u32[]{:S(2)}, u32[]{:S(2)}) collective-permute-start(f32[1,2048]{1,0:T(1,128)S(1)} %add_negate_fusion.r_ref), channel_id=1, source_target_pairs={{0,24},{8,16},{16,8},{24,0},{1,25},{9,17},{17,9},{25,1},{2,26},{10... | collective-permute-start | bytes 24584 | tf_op jit(solution)/shard_map/ppermute | solution.py:521
  166.9 18.3 %own_plan.1 = (f32[2048,768]{1,0:T(8,128)}, f32[2048,128]{1,0:T(8,128)}) custom-call(bf16[2048,768]{1,0:T(8,128)(2,1)} %refs_1_.1, f32[1,2048]{1,0:T(1,128)S(1)} %copy-done.3, bf16[2048,768]{1,0:T(8,128)(2,1)} %v_ref.3, f32[1,2048]{1,0:T(1,128)S(1)} %add_negate_fusion.r_ref), custom_call_target="tpu_custom_call" | custom-call | flops 12884901888 | bytes 6291456 | tf_op jit(solution)/shard_map/own_plan/pallas_call | solution.py:327
  185.3 50.7 %new_centroids.1 = (bf16[2048,768]{1,0:T(8,128)(2,1)}, bf16[64,768]{1,0:T(8,128)(2,1)S(1)}, bf16[64,768]{1,0:T(8,128)(2,1)S(1)}, bf16[64,768]{1,0:T(8,128)(2,1)S...) custom-call(s32[1]{0:T(128)} %bitcast.refs_0_, ...), custom_call_target="tpu_custom_call" | custom-call | flops 38654705664 | bytes 9437184 | tf_op jit(solution)/shard_map/new_centroids/pallas_call | solution.py:429
  236.1 1.6 collective-permute-start.40
  237.9 1.5 collective-permute-start.42
  239.6 2.5 collective-permute-start.44
  242.1 0.8 collective-permute-start.45
  243.5 5.2 %collective-permute-done.43.refs_7_ = bf16[64,768]{1,0:T(8,128)(2,1)S(1)} collective-permute-done((bf16[64,768]{1,0:T(8,128)(2,1)S(1)}, bf16[64,768]{1,0:T(8,128)(2,1)S(1)}, u32[]{:S(2)}, u32[]{:S(2)}) %collective-permute-start.43) | collective-permute-done | bytes 98336 | tf_op jit(solution)/shard_map/ppermute | solution.py:521
  248.8 1.2 subtract_rows.1
  (72 shorter events, 4.5 us)
Async XLA Ops:
  0.6 22.5 %copy-start.5 = (s32[256]{0:T(256)S(1)}, s32[256]{0:T(256)}, u32[]{:S(2)}) copy-start(s32[256]{0:T(256)} %param.5) | copy-start | bytes 3076
  11.7 5.8 %copy-start = (f32[2048,2048]{1,0:T(8,128)}, f32[2048,2048]{1,0:T(8,128)S(1)}, u32[]{:S(2)}) copy-start(f32[2048,2048]{1,0:T(8,128)S(1)} %get-tuple-element.33.refs_0_) | copy-start | bytes 50331652
  17.5 6.2 %collective-permute-start = (f32[2,2048]{1,0:T(2,128)S(1)}, f32[2,2048]{1,0:T(2,128)S(1)}, u32[]{:S(2)}, u32[]{:S(2)}) collective-permute-start(f32[2,2048]{1,0:T(2,128)S(1)} %get-tuple-element.34.refs_2_), channel_id=1, source_target_pairs={{0,8},{8,0},{16,24},{24,16},{1,9},{9,1},{17,25},{25,17},{2,10},{10... | collective-permute-start | bytes 49160 | tf_op jit(solution)/shard_map/ppermute | solution.py:521
  20.5 4.7 %collective-permute-start.1 = (f32[2,2048]{1,0:T(2,128)S(1)}, f32[2,2048]{1,0:T(2,128)S(1)}, u32[]{:S(2)}, u32[]{:S(2)}) collective-permute-start(f32[2,2048]{1,0:T(2,128)S(1)} %get-tuple-element.34.refs_2_), channel_id=1, source_target_pairs={{0,16},{8,24},{16,0},{24,8},{1,17},{9,25},{17,1},{25,9},{2,18},{10... | collective-permute-start | bytes 49160 | tf_op jit(solution)/shard_map/ppermute | solution.py:521
  23.1 5.5 %collective-permute-start.2 = (f32[2,2048]{1,0:T(2,128)S(1)}, f32[2,2048]{1,0:T(2,128)S(1)}, u32[]{:S(2)}, u32[]{:S(2)}) collective-permute-start(f32[2,2048]{1,0:T(2,128)S(1)} %get-tuple-element.34.refs_2_), channel_id=1, source_target_pairs={{0,24},{8,16},{16,8},{24,0},{1,25},{9,17},{17,9},{25,1},{2,26},{10... | collective-permute-start | bytes 49160 | tf_op jit(solution)/shard_map/ppermute | solution.py:521
  28.7 5.8 %copy-start.1 = (f32[2048,2048]{1,0:T(8,128)S(1)}, f32[2048,2048]{1,0:T(8,128)}, u32[]{:S(2)}) copy-start(f32[2048,2048]{1,0:T(8,128)} %copy-done) | copy-start | bytes 50331652
  41.5 1.2 collective-permute-start.3
  42.5 29.5 %collective-permute-start.24 = (bf16[256,768]{1,0:T(8,128)(2,1)S(1)}, bf16[256,768]{1,0:T(8,128)(2,1)S(1)}, u32[]{:S(2)}, u32[]{:S(2)}) collective-permute-start(bf16[256,768]{1,0:T(8,128)(2,1)S(1)} %constant_dynamic-slice_fusion.refs_1_), channel_id=1, source_target_pairs={{0,8},{8,0},{16,24},{24,16},{1,9},{9,1},{17,25},{25,17},{2,10},{10... | collective-permute-start | bytes 1179656 | tf_op jit(solution)/shard_map/ppermute | solution.py:521
  42.8 4.0 %collective-permute-start.4 = (f32[4,2048]{1,0:T(4,128)S(1)}, f32[4,2048]{1,0:T(4,128)S(1)}, u32[]{:S(2)}, u32[]{:S(2)}) collective-permute-start(f32[4,2048]{1,0:T(4,128)S(1)} %pad_maximum_fusion.refs_2_), channel_id=1, source_target_pairs={{0,2},{1,3},{2,0},{3,1},{4,6},{5,7},{6,4},{7,5},{8,10},{9,11},{10,... | collective-permute-start | bytes 98312 | tf_op jit(solution)/shard_map/ppermute | solution.py:521
  44.3 3.9 %collective-permute-start.5 = (f32[4,2048]{1,0:T(4,128)S(1)}, f32[4,2048]{1,0:T(4,128)S(1)}, u32[]{:S(2)}, u32[]{:S(2)}) collective-permute-start(f32[4,2048]{1,0:T(4,128)S(1)} %pad_maximum_fusion.refs_2_), channel_id=1, source_target_pairs={{0,4},{1,5},{2,6},{3,7},{4,0},{5,1},{6,2},{7,3},{8,12},{9,13},{10,... | collective-permute-start | bytes 98312 | tf_op jit(solution)/shard_map/ppermute | solution.py:521
  45.8 4.8 %collective-permute-start.6 = (f32[4,2048]{1,0:T(4,128)S(1)}, f32[4,2048]{1,0:T(4,128)S(1)}, u32[]{:S(2)}, u32[]{:S(2)}) collective-permute-start(f32[4,2048]{1,0:T(4,128)S(1)} %pad_maximum_fusion.refs_2_), channel_id=1, source_target_pairs={{0,6},{1,7},{2,4},{3,5},{4,2},{5,3},{6,0},{7,1},{8,14},{9,15},{10,... | collective-permute-start | bytes 98312 | tf_op jit(solution)/shard_map/ppermute | solution.py:521
  53.0 4.9 %collective-permute-start.7 = (f32[1,2048]{1,0:T(1,128)S(1)}, f32[1,2048]{1,0:T(1,128)S(1)}, u32[]{:S(2)}, u32[]{:S(2)}) collective-permute-start(f32[1,2048]{1,0:T(1,128)S(1)} %get-tuple-element.41.refs_4_), channel_id=1, source_target_pairs={{0,8},{8,0},{16,24},{24,16},{1,9},{9,1},{17,25},{25,17},{2,10},{10... | collective-permute-start | bytes 24584 | tf_op jit(solution)/shard_map/ppermute | solution.py:521
  54.9 17.1 %collective-permute-start.8 = (f32[1,2048]{1,0:T(1,128)S(1)}, f32[1,2048]{1,0:T(1,128)S(1)}, u32[]{:S(2)}, u32[]{:S(2)}) collective-permute-start(f32[1,2048]{1,0:T(1,128)S(1)} %get-tuple-element.41.refs_4_), channel_id=1, source_target_pairs={{0,16},{8,24},{16,0},{24,8},{1,17},{9,25},{17,1},{25,9},{2,18},{10... | collective-permute-start | bytes 24584 | tf_op jit(solution)/shard_map/ppermute | solution.py:521
  54.9 17.1 %collective-permute-start.9 = (f32[1,2048]{1,0:T(1,128)S(1)}, f32[1,2048]{1,0:T(1,128)S(1)}, u32[]{:S(2)}, u32[]{:S(2)}) collective-permute-start(f32[1,2048]{1,0:T(1,128)S(1)} %get-tuple-element.41.refs_4_), channel_id=1, source_target_pairs={{0,24},{8,16},{16,8},{24,0},{1,25},{9,17},{17,9},{25,1},{2,26},{10... | collective-permute-start | bytes 24584 | tf_op jit(solution)/shard_map/ppermute | solution.py:521
  57.4 53.8 %collective-permute-start.29 = (bf16[256,768]{1,0:T(8,128)(2,1)S(1)}, bf16[256,768]{1,0:T(8,128)(2,1)S(1)}, u32[]{:S(2)}, u32[]{:S(2)}) collective-permute-start(bf16[256,768]{1,0:T(8,128)(2,1)S(1)} %constant_dynamic-slice_fusion.refs_1_), channel_id=1, source_target_pairs={{0,16},{8,24},{16,0},{24,8},{1,17},{9,25},{17,1},{25,9},{2,18},{10... | collective-permute-start | bytes 1179656 | tf_op jit(solution)/shard_map/ppermute | solution.py:521
  72.0 41.6 %collective-permute-start.34 = (bf16[256,768]{1,0:T(8,128)(2,1)S(1)}, bf16[256,768]{1,0:T(8,128)(2,1)S(1)}, u32[]{:S(2)}, u32[]{:S(2)}) collective-permute-start(bf16[256,768]{1,0:T(8,128)(2,1)S(1)} %constant_dynamic-slice_fusion.refs_1_), channel_id=1, source_target_pairs={{0,24},{8,16},{16,8},{24,0},{1,25},{9,17},{17,9},{25,1},{2,26},{10... | collective-permute-start | bytes 1179656 | tf_op jit(solution)/shard_map/ppermute | solution.py:521
  72.0 42.7 %collective-permute-start.25 = (bf16[256,768]{1,0:T(8,128)(2,1)S(1)}, bf16[256,768]{1,0:T(8,128)(2,1)S(1)}, u32[]{:S(2)}, u32[]{:S(2)}) collective-permute-start(bf16[256,768]{1,0:T(8,128)(2,1)S(1)} %collective-permute-done.24.refs_0_), channel_id=1, source_target_pairs={{0,2},{1,3},{2,0},{3,1},{4,6},{5,7},{6,4},{7,5},{8,10},{9,11},{10,... | collective-permute-start | bytes 1179656 | tf_op jit(solution)/shard_map/ppermute | solution.py:521
  72.6 44.5 %collective-permute-start.26 = (bf16[256,768]{1,0:T(8,128)(2,1)S(1)}, bf16[256,768]{1,0:T(8,128)(2,1)S(1)}, u32[]{:S(2)}, u32[]{:S(2)}) collective-permute-start(bf16[256,768]{1,0:T(8,128)(2,1)S(1)} %collective-permute-done.24.refs_0_), channel_id=1, source_target_pairs={{0,4},{1,5},{2,6},{3,7},{4,0},{5,1},{6,2},{7,3},{8,12},{9,13},{10,... | collective-permute-start | bytes 1179656 | tf_op jit(solution)/shard_map/ppermute | solution.py:521
  76.3 1.2 collective-permute-start.10
  77.5 3.7 %collective-permute-start.11 = (f32[1,2048]{1,0:T(1,128)S(1)}, f32[1,2048]{1,0:T(1,128)S(1)}, u32[]{:S(2)}, u32[]{:S(2)}) collective-permute-start(f32[1,2048]{1,0:T(1,128)S(1)} %add.37.refs_2_), channel_id=1, source_target_pairs={{0,2},{1,3},{2,0},{3,1},{4,6},{5,7},{6,4},{7,5},{8,10},{9,11},{10,... | collective-permute-start | bytes 24584 | tf_op jit(solution)/shard_map/ppermute | solution.py:521
  81.2 3.7 %collective-permute-start.12 = (f32[1,2048]{1,0:T(1,128)S(1)}, f32[1,2048]{1,0:T(1,128)S(1)}, u32[]{:S(2)}, u32[]{:S(2)}) collective-permute-start(f32[1,2048]{1,0:T(1,128)S(1)} %add.37.refs_2_), channel_id=1, source_target_pairs={{0,4},{1,5},{2,6},{3,7},{4,0},{5,1},{6,2},{7,3},{8,12},{9,13},{10,... | collective-permute-start | bytes 24584 | tf_op jit(solution)/shard_map/ppermute | solution.py:521
  84.8 4.5 %collective-permute-start.13 = (f32[1,2048]{1,0:T(1,128)S(1)}, f32[1,2048]{1,0:T(1,128)S(1)}, u32[]{:S(2)}, u32[]{:S(2)}) collective-permute-start(f32[1,2048]{1,0:T(1,128)S(1)} %add.37.refs_2_), channel_id=1, source_target_pairs={{0,6},{1,7},{2,4},{3,5},{4,2},{5,3},{6,0},{7,1},{8,14},{9,15},{10,... | collective-permute-start | bytes 24584 | tf_op jit(solution)/shard_map/ppermute | solution.py:521
  91.7 3.7 %collective-permute-start.14 = (f32[1,2048]{1,0:T(1,128)S(1)}, f32[1,2048]{1,0:T(1,128)S(1)}, u32[]{:S(2)}, u32[]{:S(2)}) collective-permute-start(f32[1,2048]{1,0:T(1,128)S(1)} %column_sums.3.refs_4_), channel_id=1, source_target_pairs={{0,8},{8,0},{16,24},{24,16},{1,9},{9,1},{17,25},{25,17},{2,10},{10... | collective-permute-start | bytes 24584 | tf_op jit(solution)/shard_map/ppermute | solution.py:521
  95.3 4.5 %collective-permute-start.15 = (f32[1,2048]{1,0:T(1,128)S(1)}, f32[1,2048]{1,0:T(1,128)S(1)}, u32[]{:S(2)}, u32[]{:S(2)}) collective-permute-start(f32[1,2048]{1,0:T(1,128)S(1)} %column_sums.3.refs_4_), channel_id=1, source_target_pairs={{0,16},{8,24},{16,0},{24,8},{1,17},{9,25},{17,1},{25,9},{2,18},{10... | collective-permute-start | bytes 24584 | tf_op jit(solution)/shard_map/ppermute | solution.py:521
  99.9 5.4 %collective-permute-start.16 = (f32[1,2048]{1,0:T(1,128)S(1)}, f32[1,2048]{1,0:T(1,128)S(1)}, u32[]{:S(2)}, u32[]{:S(2)}) collective-permute-start(f32[1,2048]{1,0:T(1,128)S(1)} %column_sums.3.refs_4_), channel_id=1, source_target_pairs={{0,24},{8,16},{16,8},{24,0},{1,25},{9,17},{17,9},{25,1},{2,26},{10... | collective-permute-start | bytes 24584 | tf_op jit(solution)/shard_map/ppermute | solution.py:521
  111.2 3.0 %collective-permute-start.17 = (f32[1,2048]{1,0:T(1,128)S(1)}, f32[1,2048]{1,0:T(1,128)S(1)}, u32[]{:S(2)}, u32[]{:S(2)}) collective-permute-start(f32[1,2048]{1,0:T(1,128)S(1)} %get-tuple-element.45), channel_id=1, source_target_pairs={{0,1},{1,0},{2,3},{3,2},{4,5},{5,4},{6,7},{7,6},{8,9},{9,8},{10,11... | collective-permute-start | bytes 24584 | tf_op jit(solution)/shard_map/ppermute | solution.py:521
  111.2 12.9 %collective-permute-start.27 = (bf16[256,768]{1,0:T(8,128)(2,1)S(1)}, bf16[256,768]{1,0:T(8,128)(2,1)S(1)}, u32[]{:S(2)}, u32[]{:S(2)}) collective-permute-start(bf16[256,768]{1,0:T(8,128)(2,1)S(1)} %collective-permute-done.24.refs_0_), channel_id=1, source_target_pairs={{0,6},{1,7},{2,4},{3,5},{4,2},{5,3},{6,0},{7,1},{8,14},{9,15},{10,... | collective-permute-start | bytes 1179656 | tf_op jit(solution)/shard_map/ppermute | solution.py:521
  113.6 19.0 %collective-permute-start.30 = (bf16[256,768]{1,0:T(8,128)(2,1)S(1)}, bf16[256,768]{1,0:T(8,128)(2,1)S(1)}, u32[]{:S(2)}, u32[]{:S(2)}) collective-permute-start(bf16[256,768]{1,0:T(8,128)(2,1)S(1)} %collective-permute-done.29.refs_0_), channel_id=1, source_target_pairs={{0,2},{1,3},{2,0},{3,1},{4,6},{5,7},{6,4},{7,5},{8,10},{9,11},{10,... | collective-permute-start | bytes 1179656 | tf_op jit(solution)/shard_map/ppermute | solution.py:521
  114.2 19.9 %collective-permute-start.31 = (bf16[256,768]{1,0:T(8,128)(2,1)S(1)}, bf16[256,768]{1,0:T(8,128)(2,1)S(1)}, u32[]{:S(2)}, u32[]{:S(2)}) collective-permute-start(bf16[256,768]{1,0:T(8,128)(2,1)S(1)} %collective-permute-done.29.refs_0_), channel_id=1, source_target_pairs={{0,4},{1,5},{2,6},{3,7},{4,0},{5,1},{6,2},{7,3},{8,12},{9,13},{10,... | collective-permute-start | bytes 1179656 | tf_op jit(solution)/shard_map/ppermute | solution.py:521
  114.7 26.3 %collective-permute-start.32 = (bf16[256,768]{1,0:T(8,128)(2,1)S(1)}, bf16[256,768]{1,0:T(8,128)(2,1)S(1)}, u32[]{:S(2)}, u32[]{:S(2)}) collective-permute-start(bf16[256,768]{1,0:T(8,128)(2,1)S(1)} %collective-permute-done.29.refs_0_), channel_id=1, source_target_pairs={{0,6},{1,7},{2,4},{3,5},{4,2},{5,3},{6,0},{7,1},{8,14},{9,15},{10,... | collective-permute-start | bytes 1179656 | tf_op jit(solution)/shard_map/ppermute | solution.py:521
  117.1 32.4 %collective-permute-start.35 = (bf16[256,768]{1,0:T(8,128)(2,1)S(1)}, bf16[256,768]{1,0:T(8,128)(2,1)S(1)}, u32[]{:S(2)}, u32[]{:S(2)}) collective-permute-start(bf16[256,768]{1,0:T(8,128)(2,1)S(1)} %collective-permute-done.34.refs_0_), channel_id=1, source_target_pairs={{0,2},{1,3},{2,0},{3,1},{4,6},{5,7},{6,4},{7,5},{8,10},{9,11},{10,... | collective-permute-start | bytes 1179656 | tf_op jit(solution)/shard_map/ppermute | solution.py:521
  124.1 29.4 %collective-permute-start.36 = (bf16[256,768]{1,0:T(8,128)(2,1)S(1)}, bf16[256,768]{1,0:T(8,128)(2,1)S(1)}, u32[]{:S(2)}, u32[]{:S(2)}) collective-permute-start(bf16[256,768]{1,0:T(8,128)(2,1)S(1)} %collective-permute-done.34.refs_0_), channel_id=1, source_target_pairs={{0,4},{1,5},{2,6},{3,7},{4,0},{5,1},{6,2},{7,3},{8,12},{9,13},{10,... | collective-permute-start | bytes 1179656 | tf_op jit(solution)/shard_map/ppermute | solution.py:521
  132.6 25.0 %collective-permute-start.37 = (bf16[256,768]{1,0:T(8,128)(2,1)S(1)}, bf16[256,768]{1,0:T(8,128)(2,1)S(1)}, u32[]{:S(2)}, u32[]{:S(2)}) collective-permute-start(bf16[256,768]{1,0:T(8,128)(2,1)S(1)} %collective-permute-done.34.refs_0_), channel_id=1, source_target_pairs={{0,6},{1,7},{2,4},{3,5},{4,2},{5,3},{6,0},{7,1},{8,14},{9,15},{10,... | collective-permute-start | bytes 1179656 | tf_op jit(solution)/shard_map/ppermute | solution.py:521
  134.1 24.7 %collective-permute-start.18 = (f32[1,2048]{1,0:T(1,128)S(1)}, f32[1,2048]{1,0:T(1,128)S(1)}, u32[]{:S(2)}, u32[]{:S(2)}) collective-permute-start(f32[1,2048]{1,0:T(1,128)S(1)} %add.38), channel_id=1, source_target_pairs={{0,2},{1,3},{2,0},{3,1},{4,6},{5,7},{6,4},{7,5},{8,10},{9,11},{10,... | collective-permute-start | bytes 24584 | tf_op jit(solution)/shard_map/ppermute | solution.py:521
  141.0 18.4 %collective-permute-start.19 = (f32[1,2048]{1,0:T(1,128)S(1)}, f32[1,2048]{1,0:T(1,128)S(1)}, u32[]{:S(2)}, u32[]{:S(2)}) collective-permute-start(f32[1,2048]{1,0:T(1,128)S(1)} %add.38), channel_id=1, source_target_pairs={{0,4},{1,5},{2,6},{3,7},{4,0},{5,1},{6,2},{7,3},{8,12},{9,13},{10,... | collective-permute-start | bytes 24584 | tf_op jit(solution)/shard_map/ppermute | solution.py:521
  149.5 9.9 %collective-permute-start.20 = (f32[1,2048]{1,0:T(1,128)S(1)}, f32[1,2048]{1,0:T(1,128)S(1)}, u32[]{:S(2)}, u32[]{:S(2)}) collective-permute-start(f32[1,2048]{1,0:T(1,128)S(1)} %add.38), channel_id=1, source_target_pairs={{0,6},{1,7},{2,4},{3,5},{4,2},{5,3},{6,0},{7,1},{8,14},{9,15},{10,... | collective-permute-start | bytes 24584 | tf_op jit(solution)/shard_map/ppermute | solution.py:521
  152.3 2.0 copy-start.4
  153.5 13.4 %copy-start.3 = (f32[1,2048]{1,0:T(1,128)S(1)}, f32[1,2048]{1,0:T(1,128)}, u32[]{:S(2)}) copy-start(f32[1,2048]{1,0:T(1,128)} %get-tuple-element.44.col_ref.refs_2_) | copy-start | bytes 24580
  154.3 31.0 %collective-permute-start.28 = (bf16[1024,768]{1,0:T(8,128)(2,1)S(1)}, bf16[1024,768]{1,0:T(8,128)(2,1)}, u32[]{:S(2)}, u32[]{:S(2)}) collective-permute-start(bf16[1024,768]{1,0:T(8,128)(2,1)S(1)} %copy-done.4), channel_id=1, source_target_pairs={{0,1},{1,0},{2,3},{3,2},{4,5},{5,4},{6,7},{7,6},{8,9},{9,8},{10,11... | collective-permute-start | bytes 4718600 | tf_op jit(solution)/shard_map/ppermute | solution.py:521
  157.6 27.7 %collective-permute-start.33 = (bf16[1024,768]{1,0:T(8,128)(2,1)}, bf16[1024,768]{1,0:T(8,128)(2,1)}, u32[]{:S(2)}, u32[]{:S(2)}) collective-permute-start(bf16[1024,768]{1,0:T(8,128)(2,1)} %join_pieces.4.refs_11_), channel_id=1, source_target_pairs={{0,1},{1,0},{2,3},{3,2},{4,5},{5,4},{6,7},{7,6},{8,9},{9,8},{10,11... | collective-permute-start | bytes 4718600 | tf_op jit(solution)/shard_map/ppermute | solution.py:521
  158.8 26.5 %collective-permute-start.38 = (bf16[1024,768]{1,0:T(8,128)(2,1)}, bf16[1024,768]{1,0:T(8,128)(2,1)}, u32[]{:S(2)}, u32[]{:S(2)}) collective-permute-start(bf16[1024,768]{1,0:T(8,128)(2,1)} %join_pieces.5.refs_13_), channel_id=1, source_target_pairs={{0,1},{1,0},{2,3},{3,2},{4,5},{5,4},{6,7},{7,6},{8,9},{9,8},{10,11... | collective-permute-start | bytes 4718600 | tf_op jit(solution)/shard_map/ppermute | solution.py:521
  159.4 25.8 %copy-start.2 = (f32[1,2048]{1,0:T(1,128)}, f32[1,2048]{1,0:T(1,128)S(1)}, u32[]{:S(2)}) copy-start(f32[1,2048]{1,0:T(1,128)S(1)} %add_negate_fusion.r_ref) | copy-start | bytes 24580
  159.4 4.8 %collective-permute-start.21 = (f32[1,2048]{1,0:T(1,128)S(1)}, f32[1,2048]{1,0:T(1,128)S(1)}, u32[]{:S(2)}, u32[]{:S(2)}) collective-permute-start(f32[1,2048]{1,0:T(1,128)S(1)} %add_negate_fusion.r_ref), channel_id=1, source_target_pairs={{0,8},{8,0},{16,24},{24,16},{1,9},{9,1},{17,25},{25,17},{2,10},{10... | collective-permute-start | bytes 24584 | tf_op jit(solution)/shard_map/ppermute | solution.py:521
  159.8 25.4 %collective-permute-start.22 = (f32[1,2048]{1,0:T(1,128)S(1)}, f32[1,2048]{1,0:T(1,128)S(1)}, u32[]{:S(2)}, u32[]{:S(2)}) collective-permute-start(f32[1,2048]{1,0:T(1,128)S(1)} %add_negate_fusion.r_ref), channel_id=1, source_target_pairs={{0,16},{8,24},{16,0},{24,8},{1,17},{9,25},{17,1},{25,9},{2,18},{10... | collective-permute-start | bytes 24584 | tf_op jit(solution)/shard_map/ppermute | solution.py:521
  164.2 21.0 %collective-permute-start.23 = (f32[1,2048]{1,0:T(1,128)S(1)}, f32[1,2048]{1,0:T(1,128)S(1)}, u32[]{:S(2)}, u32[]{:S(2)}) collective-permute-start(f32[1,2048]{1,0:T(1,128)S(1)} %add_negate_fusion.r_ref), channel_id=1, source_target_pairs={{0,24},{8,16},{16,8},{24,0},{1,25},{9,17},{17,9},{25,1},{2,26},{10... | collective-permute-start | bytes 24584 | tf_op jit(solution)/shard_map/ppermute | solution.py:521
  236.0 3.6 %collective-permute-start.39 = (bf16[64,768]{1,0:T(8,128)(2,1)S(1)}, bf16[64,768]{1,0:T(8,128)(2,1)S(1)}, u32[]{:S(2)}, u32[]{:S(2)}) collective-permute-start(bf16[64,768]{1,0:T(8,128)(2,1)S(1)} %get-tuple-element.55), channel_id=1, source_target_pairs={{0,1},{1,0},{2,3},{3,2},{4,5},{5,4},{6,7},{7,6},{8,9},{9,8},{10,11... | collective-permute-start | bytes 294920 | tf_op jit(solution)/shard_map/ppermute | solution.py:521
  236.1 6.0 %collective-permute-start.40 = (bf16[64,768]{1,0:T(8,128)(2,1)S(1)}, bf16[64,768]{1,0:T(8,128)(2,1)S(1)}, u32[]{:S(2)}, u32[]{:S(2)}) collective-permute-start(bf16[64,768]{1,0:T(8,128)(2,1)S(1)} %get-tuple-element.56), channel_id=1, source_target_pairs={{0,2},{1,3},{2,0},{3,1},{4,6},{5,7},{6,4},{7,5},{8,10},{9,11},{10,... | collective-permute-start | bytes 294920 | tf_op jit(solution)/shard_map/ppermute | solution.py:521
  237.6 5.4 %collective-permute-start.41 = (bf16[64,768]{1,0:T(8,128)(2,1)S(1)}, bf16[64,768]{1,0:T(8,128)(2,1)S(1)}, u32[]{:S(2)}, u32[]{:S(2)}) collective-permute-start(bf16[64,768]{1,0:T(8,128)(2,1)S(1)} %get-tuple-element.57), channel_id=1, source_target_pairs={{0,3},{1,2},{2,1},{3,0},{4,7},{5,6},{6,5},{7,4},{8,11},{9,10},{10,... | collective-permute-start | bytes 294920 | tf_op jit(solution)/shard_map/ppermute | solution.py:521
  237.9 5.6 %collective-permute-start.42 = (bf16[64,768]{1,0:T(8,128)(2,1)S(1)}, bf16[64,768]{1,0:T(8,128)(2,1)S(1)}, u32[]{:S(2)}, u32[]{:S(2)}) collective-permute-start(bf16[64,768]{1,0:T(8,128)(2,1)S(1)} %get-tuple-element.58), channel_id=1, source_target_pairs={{0,4},{1,5},{2,6},{3,7},{4,0},{5,1},{6,2},{7,3},{8,12},{9,13},{10,... | collective-permute-start | bytes 294920 | tf_op jit(solution)/shard_map/ppermute | solution.py:521
  239.5 9.3 %collective-permute-start.43 = (bf16[64,768]{1,0:T(8,128)(2,1)S(1)}, bf16[64,768]{1,0:T(8,128)(2,1)S(1)}, u32[]{:S(2)}, u32[]{:S(2)}) collective-permute-start(bf16[64,768]{1,0:T(8,128)(2,1)S(1)} %get-tuple-element.59), channel_id=1, source_target_pairs={{0,5},{1,4},{2,7},{3,6},{4,1},{5,0},{6,3},{7,2},{8,13},{9,12},{10,... | collective-permute-start | bytes 294920 | tf_op jit(solution)/shard_map/ppermute | solution.py:521
  239.6 9.1 %collective-permute-start.44 = (bf16[64,768]{1,0:T(8,128)(2,1)S(1)}, bf16[64,768]{1,0:T(8,128)(2,1)S(1)}, u32[]{:S(2)}, u32[]{:S(2)}) collective-permute-start(bf16[64,768]{1,0:T(8,128)(2,1)S(1)} %get-tuple-element.60), channel_id=1, source_target_pairs={{0,6},{1,7},{2,4},{3,5},{4,2},{5,3},{6,0},{7,1},{8,14},{9,15},{10,... | collective-permute-start | bytes 294920 | tf_op jit(solution)/shard_map/ppermute | solution.py:521
  242.1 6.7 %collective-permute-start.45 = (bf16[64,768]{1,0:T(8,128)(2,1)S(1)}, bf16[64,768]{1,0:T(8,128)(2,1)S(1)}, u32[]{:S(2)}, u32[]{:S(2)}) collective-permute-start(bf16[64,768]{1,0:T(8,128)(2,1)S(1)} %get-tuple-element.61), channel_id=1, source_target_pairs={{0,7},{1,6},{2,5},{3,4},{4,3},{5,2},{6,1},{7,0},{8,15},{9,14},{10,... | collective-permute-start | bytes 294920 | tf_op jit(solution)/shard_map/ppermute | solution.py:521

commit v2 on v1

--- a/solution.py
+++ b/solution.py
@@ -95,7 +95,7 @@
 def first_rows_kernel(*refs, parts, log_mass, group):
     l_ref, ids_ref = refs[0:2]
     stats = refs[2 : 2 + parts]
-    m_ref, stat_ref, col_ref, spare_ref, peaks, totals = refs[2 + parts :]
+    m_ref, stat_ref, col_ref, peaks, totals = refs[2 + parts :]
 
     @pl.when(pl.program_id(0) == 0)
     def _():
@@ -111,7 +111,6 @@
         scaled = jnp.exp(shifted - peak)
         rounded = scaled.astype(BF16)
         m_ref[rows, :] = rounded
-        spare_ref[rows, :] = rounded
         peaks[rows, :] = jnp.broadcast_to(peak, (group, 128))
         totals[rows, :] = jnp.broadcast_to(jnp.sum(scaled, axis=1, keepdims=True), (group, 128))
         return carry
@@ -137,13 +136,11 @@
             pl.BlockSpec((tile, lists), lambda i: (i, 0)),
             pl.BlockSpec((3, tile), lambda i: (0, i)),
             whole((1, lists)),
-            pl.BlockSpec((tile, lists), lambda i: (i, 0)),
         ],
         out_shape=[
             pltpu.VMEM((rows, lists), BF16),
             jax.ShapeDtypeStruct((3, rows), F32),
             jax.ShapeDtypeStruct((1, lists), F32),
-            pltpu.HBM((rows, lists), BF16),
         ],
         scratch_shapes=[pltpu.VMEM((tile, 128), F32), pltpu.VMEM((tile, 128), F32)],
         compiler_params=grant(24),
@@ -261,28 +258,29 @@
         compiler_params=grant(16),
         cost_estimate=cost(16 * rows * lists, 2 * rows * lists),
         name="row_sums",
-    )(in_hbm(scaled) if last else in_vmem(scaled), first_column, own, peak, *stats)
+    )(in_vmem(scaled), first_column, own, peak, *stats)
 
 
 def block_sums(blocks):
     flat = [(index, item) for index, block in enumerate(blocks) for item in block]
 
     def logits(item):
-        return lax.dot_general(item[0], item[2](), NT, preferred_element_type=F32)
+        here = item[2]()
+        return here, lax.dot_general(item[0], here, NT, preferred_element_type=F32)
 
     found = [None] * len(blocks)
-    ready = logits(flat[0][1])
+    here, ready = logits(flat[0][1])
     for place, (index, item) in enumerate(flat):
-        following = logits(flat[place + 1][1]) if place + 1 < len(flat) else None
+        following = logits(flat[place + 1][1]) if place + 1 < len(flat) else (None, None)
         plan = jnp.exp(ready + item[3]() + item[1]).astype(BF16)
-        part = lax.dot_general(plan, item[2](), NN, preferred_element_type=F32)
+        part = lax.dot_general(plan, here, NN, preferred_element_type=F32)
         wide = plan.astype(F32)
         sums = wide[:, 0:128]
         for lane in range(128, wide.shape[1], 128):
             sums = sums + wide[:, lane : lane + 128]
         before = found[index]
         found[index] = (part, sums) if before is None else (before[0] + part, before[1] + sums)
-        ready = following
+        here, ready = following
     return found
 
 
@@ -376,7 +374,14 @@
         here = held.at[pl.ds((key - 1) * count, count)]
         pltpu.make_async_copy(here, here, sems.at[key - 1]).wait()
 
-    def compute():
+    def arriving(key):
+        def load():
+            wait(key)
+            return held[chunk((key - 1) * (count // depth), depth), :]
+
+        return load
+
+    def compute(staged):
         doubled, column = c_ref[...] * 2, wide_column(col_ref)
         steps = count // depth
         every = slice(None)
@@ -385,7 +390,9 @@
                 (
                     doubled,
                     column,
-                    loads(held, chunk((key - 1) * steps + step, depth), every),
+                    arriving(key)
+                    if staged and step == 0
+                    else loads(held, chunk((key - 1) * steps + step, depth), every),
                     loads(rows_in[key - 1], every, chunk(step, depth)),
                 )
                 for step in range(steps)
@@ -411,7 +418,7 @@
         for key in range(1, planes):
             wait(key)
 
-    chosen[...] += compute()
+    chosen[...] += compute(False)
 
     @pl.when(turn == pl.num_programs(0) - 1)
     def _():
@@ -424,7 +431,7 @@
     lists, width = centroids.shape
     others = len(rows)
     count = rows[0].shape[1]
-    tile, depth = min(256, lists), min(1024, count)
+    tile, depth = min(512, lists), min(1024, count)
     total = others * count
     return pl.pallas_call(
         functools.partial(plan_kernel, planes=others + 1, owners=owners, depth=depth),
@@ -459,7 +466,7 @@
         in_hbm(masses),
         ids,
         *rows,
-        *[in_hbm(half) for half in halves],
+        *halves,
     )
 
 
@@ -565,7 +572,7 @@
     if data_count > 2:
         arriving.append(swap(after(own, *parts), "dp", 2))
     moved = across(arriving[0], stats)
-    scaled, own_stats, first_column, spare = first_rows(logits, ids_row, parts, log_mass)
+    scaled, own_stats, first_column = first_rows(logits, ids_row, parts, log_mass)
     partner = swap(own_stats, "cent", 1)
     pair = jnp.concatenate(
         join_pairs([own_stats, partner]) + (own_stats[2:3], partner[2:3]), axis=0
@@ -582,16 +589,14 @@
         halves += partners(moved)
         moved = across(arriving[turn], pair)
         last = turn == ITERS - 1
-        sums, *kept = column_sums(scaled, own_stats, parts, last, peak)
+        sums, *kept = column_sums(scaled, own_stats, parts, False, peak)
         peak = kept.pop(0) if turn == 1 else peak
-        scaled = scaled if last else kept[0]
+        scaled = kept[0]
         parts = everywhere(sums, "dp")
         if turn == 1:
             for key in range(3, data_count):
                 arriving.append(swap(after(own, *parts), "dp", key))
-        sums, column, *kept = row_sums(
-            spare if last else scaled, first_column, own_stats, peak, parts, ratio, last
-        )
+        sums, column, *kept = row_sums(scaled, first_column, own_stats, peak, parts, ratio, last)
         scaled = scaled if last else kept[0]
         partner = swap(sums, "cent", 1)
         pair = sums + partner

time: 250 us -> 246 us (0.984)
  Pallas kernels: 106 us -> 101 us
    pallas_call x2, Pallas kernels: 8.98 us -> 6.3 us  [row_sums(): pl.pallas_call(functools.partial(row_sum_kernel, parts=len(stats), ratio=...]
    unnamed x12 -> x16, local copies, waits for them, and re-layouts: 12.3 us -> 12.3 us
  transfers between devices with their start and end apart: 46 -> 46, of which waited for: 21 -> 21; matrix products, arithmetic and copies ran while one was open for 1% -> 1% of each run, Pallas kernels for 14% -> 13%
where the time goes in v2:
time: 246 us
  Pallas kernels  101 us (41%)
  waiting for transfers between devices  73.4 us (30%)
  starting transfers between devices  55.5 us (23%)
  local copies, waits for them, and re-layouts  14 us (6%)
    ppermute x46, waiting for transfers between devices, swap(): return lax.ppermute(value, axis, [(i, i ^ key) for i in range(count)])  73.4 us
    ppermute x46, starting transfers between devices, swap(): return lax.ppermute(value, axis, [(i, i ^ key) for i in range(count)])  55.5 us
    pallas_call x1, Pallas kernels, new_centroids(): pl.pallas_call(functools.partial(plan_kernel, planes=others + 1, owners=o...  50.1 us
    pallas_call x1, Pallas kernels, own_plan(): pl.pallas_call(functools.partial(own_plan_kernel, depth=depth, part=min(2...  18.7 us
    unnamed x16, local copies, waits for them, and re-layouts  12.3 us
    pallas_call x1, Pallas kernels, logits_and_stats(): pl.pallas_call(functools.partial(logits_kernel, chunk=min(256, rows)), gr...  11.1 us
    pallas_call x2, Pallas kernels, row_sums(): pl.pallas_call(functools.partial(row_sum_kernel, parts=len(stats), ratio=...  6.3 us
    pallas_call x1, Pallas kernels, first_rows(): pl.pallas_call(functools.partial(first_rows_kernel, parts=len(stats), log...  5.81 us
  transfers between devices with their start and end apart: 46, of which 21 were waited for; matrix products, arithmetic and copies ran while one was open for 1% of the time, Pallas kernels for 13%

profile of v2, /device:TPU:0, one launch (start us, length us, event | category | flops | bytes accessed | tf_op | source)
XLA Modules:
  0.0 245.9 jit_solution(2208285191492247256)
XLA Ops:
  0.6 11.1 %logits_stats.1 = (f32[2048,2048]{1,0:T(8,128)S(1)}, f32[2,2048]{1,0:T(2,128)S(1)}) custom-call(bf16[2048,768]{1,0:T(8,128)(2,1)} %v_ref.3, bf16[2048,768]{1,0:T(8,128)(2,1)} %refs_1_.1), custom_call_target="tpu_custom_call" | custom-call | flops 6442450944 | bytes 16777216 | tf_op jit(solution)/shard_map/logits_stats/pallas_call | solution.py:77
  11.7 5.8 %copy-done = f32[2048,2048]{1,0:T(8,128)} copy-done((f32[2048,2048]{1,0:T(8,128)}, f32[2048,2048]{1,0:T(8,128)S(1)}, u32[]{:S(2)}) %copy-start) | copy-done | bytes 16777240
  17.5 3.1 %collective-permute-start = (f32[2,2048]{1,0:T(2,128)S(1)}, f32[2,2048]{1,0:T(2,128)S(1)}, u32[]{:S(2)}, u32[]{:S(2)}) collective-permute-start(f32[2,2048]{1,0:T(2,128)S(1)} %get-tuple-element.35.refs_2_), channel_id=1, source_target_pairs={{0,8},{8,0},{16,24},{24,16},{1,9},{9,1},{17,25},{25,17},{2,10},{10... | collective-permute-start | bytes 49160 | tf_op jit(solution)/shard_map/ppermute | solution.py:528
  20.6 2.6 %collective-permute-start.1 = (f32[2,2048]{1,0:T(2,128)S(1)}, f32[2,2048]{1,0:T(2,128)S(1)}, u32[]{:S(2)}, u32[]{:S(2)}) collective-permute-start(f32[2,2048]{1,0:T(2,128)S(1)} %get-tuple-element.35.refs_2_), channel_id=1, source_target_pairs={{0,16},{8,24},{16,0},{24,8},{1,17},{9,25},{17,1},{25,9},{2,18},{10... | collective-permute-start | bytes 49160 | tf_op jit(solution)/shard_map/ppermute | solution.py:528
  23.7 1.6 collective-permute-done.1.refs_4_
  25.3 3.4 %collective-permute-done.2.refs_5_ = f32[2,2048]{1,0:T(2,128)S(1)} collective-permute-done((f32[2,2048]{1,0:T(2,128)S(1)}, f32[2,2048]{1,0:T(2,128)S(1)}, u32[]{:S(2)}, u32[]{:S(2)}) %collective-permute-start.2) | collective-permute-done | bytes 16416 | tf_op jit(solution)/shard_map/ppermute | solution.py:528
  28.7 5.8 %copy-done.1 = f32[2048,2048]{1,0:T(8,128)S(1)} copy-done((f32[2048,2048]{1,0:T(8,128)S(1)}, f32[2048,2048]{1,0:T(8,128)}, u32[]{:S(2)}) %copy-start.1) | copy-done | bytes 16777240
  34.5 5.8 %first_rows.1 = (bf16[2048,2048]{1,0:T(8,128)(2,1)S(1)}, f32[3,2048]{1,0:T(4,128)S(1)}, f32[1,2048]{1,0:T(1,128)S(1)}) custom-call(f32[2048,2048]{1,0:T(8,128)S(1)} %copy-done.1, f32[1,2048]{1,0:T(1,128)S(1)} %bitcast.21, f32[2,2048]{1,0:T(2,128)S(1)} %get-tuple-element.35.refs_2_, f32[2,2048]{1,0:T(2,128)S(1)} %collective-permute-done.refs_3_, ...), custom_call_target="tpu_custom_call" | custom-call | flops 16777216 | bytes 25165824 | tf_op jit(solution)/shard_map/first_rows/pallas_call | solution.py:127
  40.4 1.0 constant_dynamic-slice_fusion.refs_1_
  41.6 1.6 collective-permute-start.4
  43.2 1.5 collective-permute-start.5
  45.6 1.5 collective-permute-done.5.refs_4_
  47.1 2.4 collective-permute-done.6.refs_5_
  49.5 2.3 column_sums.2
  51.9 1.9 collective-permute-start.7
  53.8 2.5 collective-permute-start.9
  56.7 14.1 %collective-permute-done.8.refs_6_ = f32[1,2048]{1,0:T(1,128)S(1)} collective-permute-done((f32[1,2048]{1,0:T(1,128)S(1)}, f32[1,2048]{1,0:T(1,128)S(1)}, u32[]{:S(2)}, u32[]{:S(2)}) %collective-permute-start.8) | collective-permute-done | bytes 8224 | tf_op jit(solution)/shard_map/ppermute | solution.py:528
  70.9 0.6 collective-permute-start.25
  72.0 3.2 %row_sums.2 = (f32[1,2048]{1,0:T(1,128)S(1)}, f32[1,2048]{1,0:T(1,128)}, bf16[2048,2048]{1,0:T(8,128)(2,1)S(1)}) custom-call(bf16[2048,2048]{1,0:T(8,128)(2,1)S(1)} %get-tuple-element.38.refs_0_, f32[1,2048]{1,0:T(1,128)S(1)} %get-tuple-element.39.refs_1_, f32[3,2048]{1,0:T(4,128)S(1)} %get-tuple-element.37.refs_1_.refs_2_, ...), custom_call_target="tpu_custom_call", output_to_operand_aliasing={{2}: (0, {})} | custom-call | flops 67108864 | bytes 8388608 | tf_op jit(solution)/shard_map/row_sums/pallas_call | solution.py:234
  75.2 1.2 collective-permute-done.10
  76.4 1.6 collective-permute-start.11
  77.9 2.2 collective-permute-done.11.refs_3_
  80.1 1.5 collective-permute-start.12
  81.6 2.1 collective-permute-done.12.refs_4_
  83.7 2.4 collective-permute-start.13
  86.2 2.1 collective-permute-done.13.refs_5_
  88.3 2.3 column_sums.3
  90.6 1.1 collective-permute-start.14
  91.6 2.6 %collective-permute-done.14.refs_5_ = f32[1,2048]{1,0:T(1,128)S(1)} collective-permute-done((f32[1,2048]{1,0:T(1,128)S(1)}, f32[1,2048]{1,0:T(1,128)S(1)}, u32[]{:S(2)}, u32[]{:S(2)}) %collective-permute-start.14) | collective-permute-done | bytes 8224 | tf_op jit(solution)/shard_map/ppermute | solution.py:528
  94.2 2.3 collective-permute-start.15
  96.5 2.3 collective-permute-done.15.refs_6_
  98.8 3.8 %collective-permute-start.16 = (f32[1,2048]{1,0:T(1,128)S(1)}, f32[1,2048]{1,0:T(1,128)S(1)}, u32[]{:S(2)}, u32[]{:S(2)}) collective-permute-start(f32[1,2048]{1,0:T(1,128)S(1)} %get-tuple-element.45.refs_4_), channel_id=1, source_target_pairs={{0,24},{8,16},{16,8},{24,0},{1,25},{9,17},{17,9},{25,1},{2,26},{10... | collective-permute-start | bytes 24584 | tf_op jit(solution)/shard_map/ppermute | solution.py:528
  102.5 1.7 collective-permute-done.16.refs_7_
  104.2 3.2 %row_sums.3 = (f32[1,2048]{1,0:T(1,128)S(1)}, f32[1,2048]{1,0:T(1,128)}) custom-call(bf16[2048,2048]{1,0:T(8,128)(2,1)S(1)} %get-tuple-element.44.refs_0_, f32[1,2048]{1,0:T(1,128)S(1)} %get-tuple-element.39.refs_1_, f32[3,2048]{1,0:T(4,128)S(1)} %get-tuple-element.37.refs_1_.refs_2_, f32[1,2048]{1,0:T(1,128)S(1)} %get-tuple-element.40.refs_3_.refs_6_, ...), custom_call_target="tpu_custom_call" | custom-call | flops 67108864 | bytes 8388608 | tf_op jit(solution)/shard_map/row_sums/pallas_call | solution.py:234
  107.4 2.4 collective-permute-start.27
  109.8 0.5 collective-permute-start.30
  110.4 0.5 collective-permute-start.31
  110.9 2.4 collective-permute-start.32
  113.4 0.5 collective-permute-start.35
  114.0 6.4 %collective-permute-done.27.refs_3_ = bf16[256,768]{1,0:T(8,128)(2,1)S(1)} collective-permute-done((bf16[256,768]{1,0:T(8,128)(2,1)S(1)}, bf16[256,768]{1,0:T(8,128)(2,1)S(1)}, u32[]{:S(2)}, u32[]{:S(2)}) %collective-permute-start.27) | collective-permute-done | bytes 393248 | tf_op jit(solution)/shard_map/ppermute | solution.py:528
  120.3 1.5 collective-permute-start.36
  121.8 7.0 %collective-permute-done.30.refs_1_ = bf16[256,768]{1,0:T(8,128)(2,1)S(1)} collective-permute-done((bf16[256,768]{1,0:T(8,128)(2,1)S(1)}, bf16[256,768]{1,0:T(8,128)(2,1)S(1)}, u32[]{:S(2)}, u32[]{:S(2)}) %collective-permute-start.30) | collective-permute-done | bytes 393248 | tf_op jit(solution)/shard_map/ppermute | solution.py:528
  128.8 1.4 collective-permute-start.37
  130.3 0.6 collective-permute-start.18
  130.9 6.3 %collective-permute-done.32.refs_3_ = bf16[256,768]{1,0:T(8,128)(2,1)S(1)} collective-permute-done((bf16[256,768]{1,0:T(8,128)(2,1)S(1)}, bf16[256,768]{1,0:T(8,128)(2,1)S(1)}, u32[]{:S(2)}, u32[]{:S(2)}) %collective-permute-start.32) | collective-permute-done | bytes 393248 | tf_op jit(solution)/shard_map/ppermute | solution.py:528
  137.2 1.5 collective-permute-start.19
  138.7 7.0 %collective-permute-done.35.refs_1_ = bf16[256,768]{1,0:T(8,128)(2,1)S(1)} collective-permute-done((bf16[256,768]{1,0:T(8,128)(2,1)S(1)}, bf16[256,768]{1,0:T(8,128)(2,1)S(1)}, u32[]{:S(2)}, u32[]{:S(2)}) %collective-permute-start.35) | collective-permute-done | bytes 393248 | tf_op jit(solution)/shard_map/ppermute | solution.py:528
  145.7 1.4 collective-permute-start.20
  147.2 1.2 join_pieces.3.refs_9_
  148.4 1.2 join_pieces.4.refs_11_
  149.7 0.7 copy-done.2
  150.4 3.5 %collective-permute-done.37.refs_3_ = bf16[256,768]{1,0:T(8,128)(2,1)S(1)} collective-permute-done((bf16[256,768]{1,0:T(8,128)(2,1)S(1)}, bf16[256,768]{1,0:T(8,128)(2,1)S(1)}, u32[]{:S(2)}, u32[]{:S(2)}) %collective-permute-start.37) | collective-permute-done | bytes 393248 | tf_op jit(solution)/shard_map/ppermute | solution.py:528
  153.8 1.2 join_pieces.5.refs_13_
  155.0 0.6 collective-permute-start.38
  156.0 4.4 %collective-permute-start.22 = (f32[1,2048]{1,0:T(1,128)S(1)}, f32[1,2048]{1,0:T(1,128)S(1)}, u32[]{:S(2)}, u32[]{:S(2)}) collective-permute-start(f32[1,2048]{1,0:T(1,128)S(1)} %add_negate_fusion.r_ref), channel_id=1, source_target_pairs={{0,16},{8,24},{16,0},{24,8},{1,17},{9,25},{17,1},{25,9},{2,18},{10... | collective-permute-start | bytes 24584 | tf_op jit(solution)/shard_map/ppermute | solution.py:528
  160.4 2.7 %collective-permute-start.23 = (f32[1,2048]{1,0:T(1,128)S(1)}, f32[1,2048]{1,0:T(1,128)S(1)}, u32[]{:S(2)}, u32[]{:S(2)}) collective-permute-start(f32[1,2048]{1,0:T(1,128)S(1)} %add_negate_fusion.r_ref), channel_id=1, source_target_pairs={{0,24},{8,16},{16,8},{24,0},{1,25},{9,17},{17,9},{25,1},{2,26},{10... | collective-permute-start | bytes 24584 | tf_op jit(solution)/shard_map/ppermute | solution.py:528
  163.1 18.7 %own_plan.1 = (f32[2048,768]{1,0:T(8,128)}, f32[2048,128]{1,0:T(8,128)}) custom-call(bf16[2048,768]{1,0:T(8,128)(2,1)} %refs_1_.1, f32[1,2048]{1,0:T(1,128)S(1)} %copy-done.6, bf16[2048,768]{1,0:T(8,128)(2,1)} %v_ref.3, f32[1,2048]{1,0:T(1,128)S(1)} %add_negate_fusion.r_ref), custom_call_target="tpu_custom_call" | custom-call | flops 12884901888 | bytes 6291456 | tf_op jit(solution)/shard_map/own_plan/pallas_call | solution.py:325
  181.9 50.1 %new_centroids.1 = (bf16[2048,768]{1,0:T(8,128)(2,1)}, bf16[64,768]{1,0:T(8,128)(2,1)S(1)}, bf16[64,768]{1,0:T(8,128)(2,1)S(1)}, bf16[64,768]{1,0:T(8,128)(2,1)S...) custom-call(s32[1]{0:T(128)} %bitcast.refs_0_, ...), custom_call_target="tpu_custom_call" | custom-call | flops 38654705664 | bytes 9437184 | tf_op jit(solution)/shard_map/new_centroids/pallas_call | solution.py:436
  232.0 1.6 collective-permute-start.40
  233.9 1.5 collective-permute-start.42
  235.6 2.5 collective-permute-start.44
  238.1 0.8 collective-permute-start.45
  239.5 5.2 %collective-permute-done.43.refs_7_ = bf16[64,768]{1,0:T(8,128)(2,1)S(1)} collective-permute-done((bf16[64,768]{1,0:T(8,128)(2,1)S(1)}, bf16[64,768]{1,0:T(8,128)(2,1)S(1)}, u32[]{:S(2)}, u32[]{:S(2)}) %collective-permute-start.43) | collective-permute-done | bytes 98336 | tf_op jit(solution)/shard_map/ppermute | solution.py:528
  244.7 1.2 subtract_rows.1
  (76 shorter events, 4.6 us)
Async XLA Ops:
  0.6 22.5 %copy-start.7 = (s32[256]{0:T(256)S(1)}, s32[256]{0:T(256)}, u32[]{:S(2)}) copy-start(s32[256]{0:T(256)} %param.5) | copy-start | bytes 3076
  11.7 5.8 %copy-start = (f32[2048,2048]{1,0:T(8,128)}, f32[2048,2048]{1,0:T(8,128)S(1)}, u32[]{:S(2)}) copy-start(f32[2048,2048]{1,0:T(8,128)S(1)} %get-tuple-element.34.refs_0_) | copy-start | bytes 50331652
  17.5 6.2 %collective-permute-start = (f32[2,2048]{1,0:T(2,128)S(1)}, f32[2,2048]{1,0:T(2,128)S(1)}, u32[]{:S(2)}, u32[]{:S(2)}) collective-permute-start(f32[2,2048]{1,0:T(2,128)S(1)} %get-tuple-element.35.refs_2_), channel_id=1, source_target_pairs={{0,8},{8,0},{16,24},{24,16},{1,9},{9,1},{17,25},{25,17},{2,10},{10... | collective-permute-start | bytes 49160 | tf_op jit(solution)/shard_map/ppermute | solution.py:528
  20.6 4.7 %collective-permute-start.1 = (f32[2,2048]{1,0:T(2,128)S(1)}, f32[2,2048]{1,0:T(2,128)S(1)}, u32[]{:S(2)}, u32[]{:S(2)}) collective-permute-start(f32[2,2048]{1,0:T(2,128)S(1)} %get-tuple-element.35.refs_2_), channel_id=1, source_target_pairs={{0,16},{8,24},{16,0},{24,8},{1,17},{9,25},{17,1},{25,9},{2,18},{10... | collective-permute-start | bytes 49160 | tf_op jit(solution)/shard_map/ppermute | solution.py:528
  23.1 5.5 %collective-permute-start.2 = (f32[2,2048]{1,0:T(2,128)S(1)}, f32[2,2048]{1,0:T(2,128)S(1)}, u32[]{:S(2)}, u32[]{:S(2)}) collective-permute-start(f32[2,2048]{1,0:T(2,128)S(1)} %get-tuple-element.35.refs_2_), channel_id=1, source_target_pairs={{0,24},{8,16},{16,8},{24,0},{1,25},{9,17},{17,9},{25,1},{2,26},{10... | collective-permute-start | bytes 49160 | tf_op jit(solution)/shard_map/ppermute | solution.py:528
  28.7 5.8 %copy-start.1 = (f32[2048,2048]{1,0:T(8,128)S(1)}, f32[2048,2048]{1,0:T(8,128)}, u32[]{:S(2)}) copy-start(f32[2048,2048]{1,0:T(8,128)} %copy-done) | copy-start | bytes 50331652
  40.3 1.3 collective-permute-start.3
  41.4 29.5 %collective-permute-start.24 = (bf16[256,768]{1,0:T(8,128)(2,1)S(1)}, bf16[256,768]{1,0:T(8,128)(2,1)S(1)}, u32[]{:S(2)}, u32[]{:S(2)}) collective-permute-start(bf16[256,768]{1,0:T(8,128)(2,1)S(1)} %constant_dynamic-slice_fusion.refs_1_), channel_id=1, source_target_pairs={{0,8},{8,0},{16,24},{24,16},{1,9},{9,1},{17,25},{25,17},{2,10},{10... | collective-permute-start | bytes 1179656 | tf_op jit(solution)/shard_map/ppermute | solution.py:528
  41.6 4.0 %collective-permute-start.4 = (f32[4,2048]{1,0:T(4,128)S(1)}, f32[4,2048]{1,0:T(4,128)S(1)}, u32[]{:S(2)}, u32[]{:S(2)}) collective-permute-start(f32[4,2048]{1,0:T(4,128)S(1)} %pad_maximum_fusion.refs_2_), channel_id=1, source_target_pairs={{0,2},{1,3},{2,0},{3,1},{4,6},{5,7},{6,4},{7,5},{8,10},{9,11},{10,... | collective-permute-start | bytes 98312 | tf_op jit(solution)/shard_map/ppermute | solution.py:528
  43.2 3.9 %collective-permute-start.5 = (f32[4,2048]{1,0:T(4,128)S(1)}, f32[4,2048]{1,0:T(4,128)S(1)}, u32[]{:S(2)}, u32[]{:S(2)}) collective-permute-start(f32[4,2048]{1,0:T(4,128)S(1)} %pad_maximum_fusion.refs_2_), channel_id=1, source_target_pairs={{0,4},{1,5},{2,6},{3,7},{4,0},{5,1},{6,2},{7,3},{8,12},{9,13},{10,... | collective-permute-start | bytes 98312 | tf_op jit(solution)/shard_map/ppermute | solution.py:528
  44.7 4.8 %collective-permute-start.6 = (f32[4,2048]{1,0:T(4,128)S(1)}, f32[4,2048]{1,0:T(4,128)S(1)}, u32[]{:S(2)}, u32[]{:S(2)}) collective-permute-start(f32[4,2048]{1,0:T(4,128)S(1)} %pad_maximum_fusion.refs_2_), channel_id=1, source_target_pairs={{0,6},{1,7},{2,4},{3,5},{4,2},{5,3},{6,0},{7,1},{8,14},{9,15},{10,... | collective-permute-start | bytes 98312 | tf_op jit(solution)/shard_map/ppermute | solution.py:528
  51.9 4.9 %collective-permute-start.7 = (f32[1,2048]{1,0:T(1,128)S(1)}, f32[1,2048]{1,0:T(1,128)S(1)}, u32[]{:S(2)}, u32[]{:S(2)}) collective-permute-start(f32[1,2048]{1,0:T(1,128)S(1)} %get-tuple-element.41.refs_4_), channel_id=1, source_target_pairs={{0,8},{8,0},{16,24},{24,16},{1,9},{9,1},{17,25},{25,17},{2,10},{10... | collective-permute-start | bytes 24584 | tf_op jit(solution)/shard_map/ppermute | solution.py:528
  53.8 17.1 %collective-permute-start.8 = (f32[1,2048]{1,0:T(1,128)S(1)}, f32[1,2048]{1,0:T(1,128)S(1)}, u32[]{:S(2)}, u32[]{:S(2)}) collective-permute-start(f32[1,2048]{1,0:T(1,128)S(1)} %get-tuple-element.41.refs_4_), channel_id=1, source_target_pairs={{0,16},{8,24},{16,0},{24,8},{1,17},{9,25},{17,1},{25,9},{2,18},{10... | collective-permute-start | bytes 24584 | tf_op jit(solution)/shard_map/ppermute | solution.py:528
  53.8 17.1 %collective-permute-start.9 = (f32[1,2048]{1,0:T(1,128)S(1)}, f32[1,2048]{1,0:T(1,128)S(1)}, u32[]{:S(2)}, u32[]{:S(2)}) collective-permute-start(f32[1,2048]{1,0:T(1,128)S(1)} %get-tuple-element.41.refs_4_), channel_id=1, source_target_pairs={{0,24},{8,16},{16,8},{24,0},{1,25},{9,17},{17,9},{25,1},{2,26},{10... | collective-permute-start | bytes 24584 | tf_op jit(solution)/shard_map/ppermute | solution.py:528
  56.3 51.1 %collective-permute-start.29 = (bf16[256,768]{1,0:T(8,128)(2,1)S(1)}, bf16[256,768]{1,0:T(8,128)(2,1)S(1)}, u32[]{:S(2)}, u32[]{:S(2)}) collective-permute-start(bf16[256,768]{1,0:T(8,128)(2,1)S(1)} %constant_dynamic-slice_fusion.refs_1_), channel_id=1, source_target_pairs={{0,16},{8,24},{16,0},{24,8},{1,17},{9,25},{17,1},{25,9},{2,18},{10... | collective-permute-start | bytes 1179656 | tf_op jit(solution)/shard_map/ppermute | solution.py:528
  70.9 38.9 %collective-permute-start.34 = (bf16[256,768]{1,0:T(8,128)(2,1)S(1)}, bf16[256,768]{1,0:T(8,128)(2,1)S(1)}, u32[]{:S(2)}, u32[]{:S(2)}) collective-permute-start(bf16[256,768]{1,0:T(8,128)(2,1)S(1)} %constant_dynamic-slice_fusion.refs_1_), channel_id=1, source_target_pairs={{0,24},{8,16},{16,8},{24,0},{1,25},{9,17},{17,9},{25,1},{2,26},{10... | collective-permute-start | bytes 1179656 | tf_op jit(solution)/shard_map/ppermute | solution.py:528
  70.9 40.0 %collective-permute-start.25 = (bf16[256,768]{1,0:T(8,128)(2,1)S(1)}, bf16[256,768]{1,0:T(8,128)(2,1)S(1)}, u32[]{:S(2)}, u32[]{:S(2)}) collective-permute-start(bf16[256,768]{1,0:T(8,128)(2,1)S(1)} %collective-permute-done.24.refs_0_), channel_id=1, source_target_pairs={{0,2},{1,3},{2,0},{3,1},{4,6},{5,7},{6,4},{7,5},{8,10},{9,11},{10,... | collective-permute-start | bytes 1179656 | tf_op jit(solution)/shard_map/ppermute | solution.py:528
  71.5 41.8 %collective-permute-start.26 = (bf16[256,768]{1,0:T(8,128)(2,1)S(1)}, bf16[256,768]{1,0:T(8,128)(2,1)S(1)}, u32[]{:S(2)}, u32[]{:S(2)}) collective-permute-start(bf16[256,768]{1,0:T(8,128)(2,1)S(1)} %collective-permute-done.24.refs_0_), channel_id=1, source_target_pairs={{0,4},{1,5},{2,6},{3,7},{4,0},{5,1},{6,2},{7,3},{8,12},{9,13},{10,... | collective-permute-start | bytes 1179656 | tf_op jit(solution)/shard_map/ppermute | solution.py:528
  75.2 1.2 collective-permute-start.10
  76.4 3.7 %collective-permute-start.11 = (f32[1,2048]{1,0:T(1,128)S(1)}, f32[1,2048]{1,0:T(1,128)S(1)}, u32[]{:S(2)}, u32[]{:S(2)}) collective-permute-start(f32[1,2048]{1,0:T(1,128)S(1)} %add.37.refs_2_), channel_id=1, source_target_pairs={{0,2},{1,3},{2,0},{3,1},{4,6},{5,7},{6,4},{7,5},{8,10},{9,11},{10,... | collective-permute-start | bytes 24584 | tf_op jit(solution)/shard_map/ppermute | solution.py:528
  80.1 3.7 %collective-permute-start.12 = (f32[1,2048]{1,0:T(1,128)S(1)}, f32[1,2048]{1,0:T(1,128)S(1)}, u32[]{:S(2)}, u32[]{:S(2)}) collective-permute-start(f32[1,2048]{1,0:T(1,128)S(1)} %add.37.refs_2_), channel_id=1, source_target_pairs={{0,4},{1,5},{2,6},{3,7},{4,0},{5,1},{6,2},{7,3},{8,12},{9,13},{10,... | collective-permute-start | bytes 24584 | tf_op jit(solution)/shard_map/ppermute | solution.py:528
  83.7 4.5 %collective-permute-start.13 = (f32[1,2048]{1,0:T(1,128)S(1)}, f32[1,2048]{1,0:T(1,128)S(1)}, u32[]{:S(2)}, u32[]{:S(2)}) collective-permute-start(f32[1,2048]{1,0:T(1,128)S(1)} %add.37.refs_2_), channel_id=1, source_target_pairs={{0,6},{1,7},{2,4},{3,5},{4,2},{5,3},{6,0},{7,1},{8,14},{9,15},{10,... | collective-permute-start | bytes 24584 | tf_op jit(solution)/shard_map/ppermute | solution.py:528
  90.6 3.7 %collective-permute-start.14 = (f32[1,2048]{1,0:T(1,128)S(1)}, f32[1,2048]{1,0:T(1,128)S(1)}, u32[]{:S(2)}, u32[]{:S(2)}) collective-permute-start(f32[1,2048]{1,0:T(1,128)S(1)} %get-tuple-element.45.refs_4_), channel_id=1, source_target_pairs={{0,8},{8,0},{16,24},{24,16},{1,9},{9,1},{17,25},{25,17},{2,10},{10... | collective-permute-start | bytes 24584 | tf_op jit(solution)/shard_map/ppermute | solution.py:528
  94.2 4.5 %collective-permute-start.15 = (f32[1,2048]{1,0:T(1,128)S(1)}, f32[1,2048]{1,0:T(1,128)S(1)}, u32[]{:S(2)}, u32[]{:S(2)}) collective-permute-start(f32[1,2048]{1,0:T(1,128)S(1)} %get-tuple-element.45.refs_4_), channel_id=1, source_target_pairs={{0,16},{8,24},{16,0},{24,8},{1,17},{9,25},{17,1},{25,9},{2,18},{10... | collective-permute-start | bytes 24584 | tf_op jit(solution)/shard_map/ppermute | solution.py:528
  98.8 5.4 %collective-permute-start.16 = (f32[1,2048]{1,0:T(1,128)S(1)}, f32[1,2048]{1,0:T(1,128)S(1)}, u32[]{:S(2)}, u32[]{:S(2)}) collective-permute-start(f32[1,2048]{1,0:T(1,128)S(1)} %get-tuple-element.45.refs_4_), channel_id=1, source_target_pairs={{0,24},{8,16},{16,8},{24,0},{1,25},{9,17},{17,9},{25,1},{2,26},{10... | collective-permute-start | bytes 24584 | tf_op jit(solution)/shard_map/ppermute | solution.py:528
  107.4 3.0 %collective-permute-start.17 = (f32[1,2048]{1,0:T(1,128)S(1)}, f32[1,2048]{1,0:T(1,128)S(1)}, u32[]{:S(2)}, u32[]{:S(2)}) collective-permute-start(f32[1,2048]{1,0:T(1,128)S(1)} %get-tuple-element.47), channel_id=1, source_target_pairs={{0,1},{1,0},{2,3},{3,2},{4,5},{5,4},{6,7},{7,6},{8,9},{9,8},{10,11... | collective-permute-start | bytes 24584 | tf_op jit(solution)/shard_map/ppermute | solution.py:528
  107.4 12.9 %collective-permute-start.27 = (bf16[256,768]{1,0:T(8,128)(2,1)S(1)}, bf16[256,768]{1,0:T(8,128)(2,1)S(1)}, u32[]{:S(2)}, u32[]{:S(2)}) collective-permute-start(bf16[256,768]{1,0:T(8,128)(2,1)S(1)} %collective-permute-done.24.refs_0_), channel_id=1, source_target_pairs={{0,6},{1,7},{2,4},{3,5},{4,2},{5,3},{6,0},{7,1},{8,14},{9,15},{10,... | collective-permute-start | bytes 1179656 | tf_op jit(solution)/shard_map/ppermute | solution.py:528
  109.8 19.0 %collective-permute-start.30 = (bf16[256,768]{1,0:T(8,128)(2,1)S(1)}, bf16[256,768]{1,0:T(8,128)(2,1)S(1)}, u32[]{:S(2)}, u32[]{:S(2)}) collective-permute-start(bf16[256,768]{1,0:T(8,128)(2,1)S(1)} %collective-permute-done.29.refs_0_), channel_id=1, source_target_pairs={{0,2},{1,3},{2,0},{3,1},{4,6},{5,7},{6,4},{7,5},{8,10},{9,11},{10,... | collective-permute-start | bytes 1179656 | tf_op jit(solution)/shard_map/ppermute | solution.py:528
  110.4 19.9 %collective-permute-start.31 = (bf16[256,768]{1,0:T(8,128)(2,1)S(1)}, bf16[256,768]{1,0:T(8,128)(2,1)S(1)}, u32[]{:S(2)}, u32[]{:S(2)}) collective-permute-start(bf16[256,768]{1,0:T(8,128)(2,1)S(1)} %collective-permute-done.29.refs_0_), channel_id=1, source_target_pairs={{0,4},{1,5},{2,6},{3,7},{4,0},{5,1},{6,2},{7,3},{8,12},{9,13},{10,... | collective-permute-start | bytes 1179656 | tf_op jit(solution)/shard_map/ppermute | solution.py:528
  110.9 26.3 %collective-permute-start.32 = (bf16[256,768]{1,0:T(8,128)(2,1)S(1)}, bf16[256,768]{1,0:T(8,128)(2,1)S(1)}, u32[]{:S(2)}, u32[]{:S(2)}) collective-permute-start(bf16[256,768]{1,0:T(8,128)(2,1)S(1)} %collective-permute-done.29.refs_0_), channel_id=1, source_target_pairs={{0,6},{1,7},{2,4},{3,5},{4,2},{5,3},{6,0},{7,1},{8,14},{9,15},{10,... | collective-permute-start | bytes 1179656 | tf_op jit(solution)/shard_map/ppermute | solution.py:528
  113.4 32.4 %collective-permute-start.35 = (bf16[256,768]{1,0:T(8,128)(2,1)S(1)}, bf16[256,768]{1,0:T(8,128)(2,1)S(1)}, u32[]{:S(2)}, u32[]{:S(2)}) collective-permute-start(bf16[256,768]{1,0:T(8,128)(2,1)S(1)} %collective-permute-done.34.refs_0_), channel_id=1, source_target_pairs={{0,2},{1,3},{2,0},{3,1},{4,6},{5,7},{6,4},{7,5},{8,10},{9,11},{10,... | collective-permute-start | bytes 1179656 | tf_op jit(solution)/shard_map/ppermute | solution.py:528
  120.3 29.3 %collective-permute-start.36 = (bf16[256,768]{1,0:T(8,128)(2,1)S(1)}, bf16[256,768]{1,0:T(8,128)(2,1)S(1)}, u32[]{:S(2)}, u32[]{:S(2)}) collective-permute-start(bf16[256,768]{1,0:T(8,128)(2,1)S(1)} %collective-permute-done.34.refs_0_), channel_id=1, source_target_pairs={{0,4},{1,5},{2,6},{3,7},{4,0},{5,1},{6,2},{7,3},{8,12},{9,13},{10,... | collective-permute-start | bytes 1179656 | tf_op jit(solution)/shard_map/ppermute | solution.py:528
  128.8 25.0 %collective-permute-start.37 = (bf16[256,768]{1,0:T(8,128)(2,1)S(1)}, bf16[256,768]{1,0:T(8,128)(2,1)S(1)}, u32[]{:S(2)}, u32[]{:S(2)}) collective-permute-start(bf16[256,768]{1,0:T(8,128)(2,1)S(1)} %collective-permute-done.34.refs_0_), channel_id=1, source_target_pairs={{0,6},{1,7},{2,4},{3,5},{4,2},{5,3},{6,0},{7,1},{8,14},{9,15},{10,... | collective-permute-start | bytes 1179656 | tf_op jit(solution)/shard_map/ppermute | solution.py:528
  130.3 24.7 %collective-permute-start.18 = (f32[1,2048]{1,0:T(1,128)S(1)}, f32[1,2048]{1,0:T(1,128)S(1)}, u32[]{:S(2)}, u32[]{:S(2)}) collective-permute-start(f32[1,2048]{1,0:T(1,128)S(1)} %add.38), channel_id=1, source_target_pairs={{0,2},{1,3},{2,0},{3,1},{4,6},{5,7},{6,4},{7,5},{8,10},{9,11},{10,... | collective-permute-start | bytes 24584 | tf_op jit(solution)/shard_map/ppermute | solution.py:528
  137.2 18.4 %collective-permute-start.19 = (f32[1,2048]{1,0:T(1,128)S(1)}, f32[1,2048]{1,0:T(1,128)S(1)}, u32[]{:S(2)}, u32[]{:S(2)}) collective-permute-start(f32[1,2048]{1,0:T(1,128)S(1)} %add.38), channel_id=1, source_target_pairs={{0,4},{1,5},{2,6},{3,7},{4,0},{5,1},{6,2},{7,3},{8,12},{9,13},{10,... | collective-permute-start | bytes 24584 | tf_op jit(solution)/shard_map/ppermute | solution.py:528
  145.7 9.9 %collective-permute-start.20 = (f32[1,2048]{1,0:T(1,128)S(1)}, f32[1,2048]{1,0:T(1,128)S(1)}, u32[]{:S(2)}, u32[]{:S(2)}) collective-permute-start(f32[1,2048]{1,0:T(1,128)S(1)} %add.38), channel_id=1, source_target_pairs={{0,6},{1,7},{2,4},{3,5},{4,2},{5,3},{6,0},{7,1},{8,14},{9,15},{10,... | collective-permute-start | bytes 24584 | tf_op jit(solution)/shard_map/ppermute | solution.py:528
  148.4 2.0 copy-start.2
  149.6 13.5 %copy-start.6 = (f32[1,2048]{1,0:T(1,128)S(1)}, f32[1,2048]{1,0:T(1,128)}, u32[]{:S(2)}) copy-start(f32[1,2048]{1,0:T(1,128)} %get-tuple-element.46.col_ref.refs_2_) | copy-start | bytes 24580
  150.4 31.4 %collective-permute-start.28 = (bf16[1024,768]{1,0:T(8,128)(2,1)S(1)}, bf16[1024,768]{1,0:T(8,128)(2,1)}, u32[]{:S(2)}, u32[]{:S(2)}) collective-permute-start(bf16[1024,768]{1,0:T(8,128)(2,1)S(1)} %copy-done.2), channel_id=1, source_target_pairs={{0,1},{1,0},{2,3},{3,2},{4,5},{5,4},{6,7},{7,6},{8,9},{9,8},{10,11... | collective-permute-start | bytes 4718600 | tf_op jit(solution)/shard_map/ppermute | solution.py:528
  153.8 28.0 %collective-permute-start.33 = (bf16[1024,768]{1,0:T(8,128)(2,1)}, bf16[1024,768]{1,0:T(8,128)(2,1)}, u32[]{:S(2)}, u32[]{:S(2)}) collective-permute-start(bf16[1024,768]{1,0:T(8,128)(2,1)} %join_pieces.4.refs_11_), channel_id=1, source_target_pairs={{0,1},{1,0},{2,3},{3,2},{4,5},{5,4},{6,7},{7,6},{8,9},{9,8},{10,11... | collective-permute-start | bytes 4718600 | tf_op jit(solution)/shard_map/ppermute | solution.py:528
  155.0 26.8 %collective-permute-start.38 = (bf16[1024,768]{1,0:T(8,128)(2,1)}, bf16[1024,768]{1,0:T(8,128)(2,1)}, u32[]{:S(2)}, u32[]{:S(2)}) collective-permute-start(bf16[1024,768]{1,0:T(8,128)(2,1)} %join_pieces.5.refs_13_), channel_id=1, source_target_pairs={{0,1},{1,0},{2,3},{3,2},{4,5},{5,4},{6,7},{7,6},{8,9},{9,8},{10,11... | collective-permute-start | bytes 4718600 | tf_op jit(solution)/shard_map/ppermute | solution.py:528
  155.6 26.2 %copy-start.5 = (f32[1,2048]{1,0:T(1,128)}, f32[1,2048]{1,0:T(1,128)S(1)}, u32[]{:S(2)}) copy-start(f32[1,2048]{1,0:T(1,128)S(1)} %add_negate_fusion.r_ref) | copy-start | bytes 24580
  155.6 4.8 %collective-permute-start.21 = (f32[1,2048]{1,0:T(1,128)S(1)}, f32[1,2048]{1,0:T(1,128)S(1)}, u32[]{:S(2)}, u32[]{:S(2)}) collective-permute-start(f32[1,2048]{1,0:T(1,128)S(1)} %add_negate_fusion.r_ref), channel_id=1, source_target_pairs={{0,8},{8,0},{16,24},{24,16},{1,9},{9,1},{17,25},{25,17},{2,10},{10... | collective-permute-start | bytes 24584 | tf_op jit(solution)/shard_map/ppermute | solution.py:528
  156.0 25.7 %collective-permute-start.22 = (f32[1,2048]{1,0:T(1,128)S(1)}, f32[1,2048]{1,0:T(1,128)S(1)}, u32[]{:S(2)}, u32[]{:S(2)}) collective-permute-start(f32[1,2048]{1,0:T(1,128)S(1)} %add_negate_fusion.r_ref), channel_id=1, source_target_pairs={{0,16},{8,24},{16,0},{24,8},{1,17},{9,25},{17,1},{25,9},{2,18},{10... | collective-permute-start | bytes 24584 | tf_op jit(solution)/shard_map/ppermute | solution.py:528
  160.4 21.4 %collective-permute-start.23 = (f32[1,2048]{1,0:T(1,128)S(1)}, f32[1,2048]{1,0:T(1,128)S(1)}, u32[]{:S(2)}, u32[]{:S(2)}) collective-permute-start(f32[1,2048]{1,0:T(1,128)S(1)} %add_negate_fusion.r_ref), channel_id=1, source_target_pairs={{0,24},{8,16},{16,8},{24,0},{1,25},{9,17},{17,9},{25,1},{2,26},{10... | collective-permute-start | bytes 24584 | tf_op jit(solution)/shard_map/ppermute | solution.py:528
  163.1 18.7 %copy-start.3 = (bf16[1024,768]{1,0:T(8,128)(2,1)S(1)}, bf16[1024,768]{1,0:T(8,128)(2,1)}, u32[]{:S(2)}) copy-start(bf16[1024,768]{1,0:T(8,128)(2,1)} %join_pieces.4.refs_11_) | copy-start | bytes 4718596
  163.1 18.7 %copy-start.4 = (bf16[1024,768]{1,0:T(8,128)(2,1)S(1)}, bf16[1024,768]{1,0:T(8,128)(2,1)}, u32[]{:S(2)}) copy-start(bf16[1024,768]{1,0:T(8,128)(2,1)} %join_pieces.5.refs_13_) | copy-start | bytes 4718596
  232.0 3.6 %collective-permute-start.39 = (bf16[64,768]{1,0:T(8,128)(2,1)S(1)}, bf16[64,768]{1,0:T(8,128)(2,1)S(1)}, u32[]{:S(2)}, u32[]{:S(2)}) collective-permute-start(bf16[64,768]{1,0:T(8,128)(2,1)S(1)} %get-tuple-element.57), channel_id=1, source_target_pairs={{0,1},{1,0},{2,3},{3,2},{4,5},{5,4},{6,7},{7,6},{8,9},{9,8},{10,11... | collective-permute-start | bytes 294920 | tf_op jit(solution)/shard_map/ppermute | solution.py:528
  232.0 6.0 %collective-permute-start.40 = (bf16[64,768]{1,0:T(8,128)(2,1)S(1)}, bf16[64,768]{1,0:T(8,128)(2,1)S(1)}, u32[]{:S(2)}, u32[]{:S(2)}) collective-permute-start(bf16[64,768]{1,0:T(8,128)(2,1)S(1)} %get-tuple-element.58), channel_id=1, source_target_pairs={{0,2},{1,3},{2,0},{3,1},{4,6},{5,7},{6,4},{7,5},{8,10},{9,11},{10,... | collective-permute-start | bytes 294920 | tf_op jit(solution)/shard_map/ppermute | solution.py:528
  233.6 5.4 %collective-permute-start.41 = (bf16[64,768]{1,0:T(8,128)(2,1)S(1)}, bf16[64,768]{1,0:T(8,128)(2,1)S(1)}, u32[]{:S(2)}, u32[]{:S(2)}) collective-permute-start(bf16[64,768]{1,0:T(8,128)(2,1)S(1)} %get-tuple-element.59), channel_id=1, source_target_pairs={{0,3},{1,2},{2,1},{3,0},{4,7},{5,6},{6,5},{7,4},{8,11},{9,10},{10,... | collective-permute-start | bytes 294920 | tf_op jit(solution)/shard_map/ppermute | solution.py:528
  233.9 5.6 %collective-permute-start.42 = (bf16[64,768]{1,0:T(8,128)(2,1)S(1)}, bf16[64,768]{1,0:T(8,128)(2,1)S(1)}, u32[]{:S(2)}, u32[]{:S(2)}) collective-permute-start(bf16[64,768]{1,0:T(8,128)(2,1)S(1)} %get-tuple-element.60), channel_id=1, source_target_pairs={{0,4},{1,5},{2,6},{3,7},{4,0},{5,1},{6,2},{7,3},{8,12},{9,13},{10,... | collective-permute-start | bytes 294920 | tf_op jit(solution)/shard_map/ppermute | solution.py:528
  235.4 9.3 %collective-permute-start.43 = (bf16[64,768]{1,0:T(8,128)(2,1)S(1)}, bf16[64,768]{1,0:T(8,128)(2,1)S(1)}, u32[]{:S(2)}, u32[]{:S(2)}) collective-permute-start(bf16[64,768]{1,0:T(8,128)(2,1)S(1)} %get-tuple-element.61), channel_id=1, source_target_pairs={{0,5},{1,4},{2,7},{3,6},{4,1},{5,0},{6,3},{7,2},{8,13},{9,12},{10,... | collective-permute-start | bytes 294920 | tf_op jit(solution)/shard_map/ppermute | solution.py:528
  235.6 9.1 %collective-permute-start.44 = (bf16[64,768]{1,0:T(8,128)(2,1)S(1)}, bf16[64,768]{1,0:T(8,128)(2,1)S(1)}, u32[]{:S(2)}, u32[]{:S(2)}) collective-permute-start(bf16[64,768]{1,0:T(8,128)(2,1)S(1)} %get-tuple-element.62), channel_id=1, source_target_pairs={{0,6},{1,7},{2,4},{3,5},{4,2},{5,3},{6,0},{7,1},{8,14},{9,15},{10,... | collective-permute-start | bytes 294920 | tf_op jit(solution)/shard_map/ppermute | solution.py:528
  238.1 6.7 %collective-permute-start.45 = (bf16[64,768]{1,0:T(8,128)(2,1)S(1)}, bf16[64,768]{1,0:T(8,128)(2,1)S(1)}, u32[]{:S(2)}, u32[]{:S(2)}) collective-permute-start(bf16[64,768]{1,0:T(8,128)(2,1)S(1)} %get-tuple-element.63), channel_id=1, source_target_pairs={{0,7},{1,6},{2,5},{3,4},{4,3},{5,2},{6,1},{7,0},{8,15},{9,14},{10,... | collective-permute-start | bytes 294920 | tf_op jit(solution)/shard_map/ppermute | solution.py:528
